TPU v7x, 768 devices: a whole 4x8x12 slice. The times are simulated.
768 devices in a mesh: dp: 32 (over y, x), row: 6 (over z_lo, core), col: 4 (over z_hi).
Axes of the slice: x: 4, y: 8, z: 12 (z_hi: 4, z_lo: 3; z = z_hi * 3 + z_lo), core: 2. Of those that a mesh axis runs over, the one named last changes fastest.
Arguments:
- attn_heads: bfloat16 [98304, 2304], P(('dp', 'col'), 'row'), may hold values from -6 to 6
- out_weight: bfloat16 [2304, 4096], P('row', 'col'), may hold values from -0.125 to 0.125
- cotangent: bfloat16 [98304, 4096], P(('dp', 'row'), 'col'), may hold values from -6 to 6
Outputs:
- head_grad: bfloat16 [98304, 2304], P(('dp', 'col'), 'row')
- weight_grad: float32 [2304, 4096], P('row', 'col')
All inputs are finite; a program needn't handle non-finite values.
Results may differ from a plain program's by a relative error of at most 0.015.
Values may be sent and summed in bfloat16 or wider, within the bound.
No kernel may reach another device: no remote copies, remote signals or barrier semaphores. Data moves between devices by JAX's collectives and lax.ppermute only.
A program may use at most 32 MiB of HBM per device.

v0:
```python
import jax
import jax.numpy as jnp
from jax import lax
from jax.experimental import pallas as pl
from jax.experimental.pallas import tpu as pltpu
from jax.sharding import Mesh, PartitionSpec as P


Y, X, ZL, CORE, ZH = 8, 4, 3, 2, 4
ROW = ZL * CORE
CHUNKS = 2
LANE = 128
XS = 4


SMEM = pl.BlockSpec(memory_space=pltpu.SMEM)
VMEM = pl.BlockSpec(memory_space=pltpu.VMEM)


def ring(n, step):
    return [(i, (i + step) % n) for i in range(n)]


def spread_pairs(k):
    pairs = []
    for row in range(ROW):
        for col in range(ZH):
            d = ZH * row + (col + k) % ZH
            pairs.append((row * ZH + col, (d % ROW) * ZH + d // ROW))
    return pairs


def gather_tokens(got, at):
    blk, feat = got[0].shape
    n = feat // CHUNKS

    def kernel(at_ref, *refs):
        outs = refs[ZH:]
        for col in range(ZH):
            k = (at_ref[0] + (ZH - col)) % ZH
            for i in range(ZH):

                @pl.when(k == i)
                def _():
                    for h in range(CHUNKS):
                        for s in range(XS):
                            to, fro = (s * ZH + col) * LANE, h * n + s * LANE
                            outs[h][:, to:to + LANE] = refs[i][:, fro:fro + LANE]

    return pl.pallas_call(
        kernel,
        out_shape=[jax.ShapeDtypeStruct((blk, ZH * n), got[0].dtype)] * CHUNKS,
        in_specs=[SMEM] + [VMEM] * ZH,
        out_specs=[VMEM] * CHUNKS,
        name="gather_tokens",
    )(at.reshape(1), *got)


def order_heads(heads, rows):
    hid = heads.shape[1]
    n = len(rows[0])
    blk = heads.shape[0] // ROW

    def kernel(rows_ref, src, *outs):
        for o, out in enumerate(outs):
            for i in range(n):
                at = pl.multiple_of(rows_ref[o * n + i] * blk, blk)
                out[:, i * blk:(i + 1) * blk] = src[pl.ds(at, blk), :].T

    return pl.pallas_call(
        kernel,
        out_shape=[jax.ShapeDtypeStruct((hid, n * blk), heads.dtype)] * len(rows),
        in_specs=[SMEM, VMEM],
        out_specs=[VMEM] * len(rows),
        name="order_heads",
    )(jnp.stack([r for group in rows for r in group]), heads)


def spread_cols(pieces, at):
    shape = pieces[0].shape

    def kernel(at_ref, *refs):
        out = refs[-1]
        for col in range(ZH):
            k = (at_ref[0] + (ZH - col)) % ZH
            for i in range(ZH):

                @pl.when(k == i)
                def _():
                    v = refs[i][...]
                    for y in range(Y):
                        out[y, col] = v

    return pl.pallas_call(
        kernel,
        out_shape=jax.ShapeDtypeStruct((Y, ZH) + shape, pieces[0].dtype),
        in_specs=[SMEM] + [VMEM] * ZH,
        out_specs=VMEM,
        name="spread_cols",
    )(at.reshape(1), *pieces)


def weight_rows(pieces):
    _, _, rows, wc = pieces.shape

    def kernel(src, out):
        for y in range(Y):
            for col in range(ZH):
                for s in range(wc // LANE):
                    to = (s * ZH + col) * LANE
                    out[y * rows:(y + 1) * rows, to:to + LANE] = src[y, col, :, s * LANE:(s + 1) * LANE]

    return pl.pallas_call(
        kernel,
        out_shape=jax.ShapeDtypeStruct((Y * rows, ZH * wc), pieces.dtype),
        in_specs=[VMEM],
        out_specs=VMEM,
        name="weight_rows",
    )(pieces)


def weight_part(heads_t, own, oth):
    hid, half = heads_t[0].shape
    n = ZH * LANE

    def kernel(a, b, c, d, out):
        acc = jnp.dot(a[...], c[...], preferred_element_type=jnp.float32)
        acc += jnp.dot(b[...], d[...], preferred_element_type=jnp.float32)
        out[0] = acc.astype(out.dtype)

    return pl.pallas_call(
        kernel,
        grid=(XS,),
        out_shape=jax.ShapeDtypeStruct((XS, hid, n), own.dtype),
        in_specs=[pl.BlockSpec((hid, half), lambda s: (0, 0))] * 2 + [pl.BlockSpec((half, n), lambda s: (0, s))] * 2,
        out_specs=pl.BlockSpec((1, hid, n), lambda s: (s, 0, 0)),
        name="weight_part",
    )(*heads_t, own, oth)


def heads_grad(owns, oths, weights, rows, at):
    half = owns[0].shape[0]
    hid, n = weights[0].shape
    blk = half // len(rows[0])
    count = len(rows[0])

    def kernel(at_ref, rows_ref, *refs):
        sides = (refs[:CHUNKS], refs[CHUNKS:2 * CHUNKS])
        w_refs, out, acc = refs[2 * CHUNKS:2 * CHUNKS + X], refs[-2], refs[-1]
        for o, side in enumerate(sides):
            for k in range(X):
                g = (at_ref[0] + (X - k)) % X
                lo = pl.multiple_of((g % 2) * n, n)
                for h in range(CHUNKS):

                    @pl.when(g // 2 == h)
                    def _():
                        prod = lax.dot_general(
                            side[h][:, pl.ds(lo, n)], w_refs[k][...], (((1,), (1,)), ((), ())),
                            preferred_element_type=jnp.float32,
                        )
                        acc[...] = prod if k == 0 else acc[...] + prod
            for i in range(count):
                to = pl.multiple_of(rows_ref[o * count + i] * blk, blk)
                out[pl.ds(to, blk), :] = acc[i * blk:(i + 1) * blk, :].astype(out.dtype)

    return pl.pallas_call(
        kernel,
        out_shape=jax.ShapeDtypeStruct((2 * half, hid), owns[0].dtype),
        in_specs=[SMEM, SMEM] + [VMEM] * (2 * CHUNKS + X),
        out_specs=VMEM,
        scratch_shapes=[pltpu.VMEM((half, hid), jnp.float32)],
        name="heads_grad",
    )(at.reshape(1), jnp.stack([r for group in rows for r in group]), *owns, *oths, *weights)


def sum_split(parts):
    rows = parts[0].shape[1] // Y

    def kernel(*refs):
        out = refs[-1]
        for h in range(CHUNKS):
            for col in range(ZH):
                v = refs[h][:, :, col * LANE:(col + 1) * LANE].astype(jnp.float32)
                out[0, col, h] = jnp.sum(v, axis=0).astype(out.dtype)

    return pl.pallas_call(
        kernel,
        grid=(Y,),
        out_shape=jax.ShapeDtypeStruct((Y, ZH, CHUNKS, rows, LANE), parts[0].dtype),
        in_specs=[pl.BlockSpec((X, rows, ZH * LANE), lambda y: (0, y, 0))] * CHUNKS,
        out_specs=pl.BlockSpec((1, ZH, CHUNKS, rows, LANE), lambda y: (y, 0, 0, 0, 0)),
        name="sum_split",
    )(*parts)


def spread_sum(parts):
    shape = parts.shape[1:]

    def kernel(src, out):
        total = jnp.sum(src[...].astype(jnp.float32), axis=0).astype(out.dtype)
        for y in range(Y):
            out[y] = total

    return pl.pallas_call(
        kernel,
        out_shape=jax.ShapeDtypeStruct((Y,) + shape, parts.dtype),
        in_specs=[VMEM],
        out_specs=VMEM,
        name="spread_sum",
    )(parts)


def spread_rows(parts):
    rows = parts.shape[2]

    def kernel(src, out):
        for x in range(X):
            for y in range(Y):
                for h in range(CHUNKS):
                    out[x, h, y * rows:(y + 1) * rows] = src[y, h]

    return pl.pallas_call(
        kernel,
        out_shape=jax.ShapeDtypeStruct((X, CHUNKS, Y * rows, LANE), parts.dtype),
        in_specs=[VMEM],
        out_specs=VMEM,
        name="spread_rows",
    )(parts)


def finish(parts, scale):
    hid = parts.shape[2]
    rows = hid // 2

    def kernel(src, out):
        for h in range(CHUNKS):
            for x in range(X):
                at = (h * X + x) * LANE
                out[:, at:at + LANE] = src[x, h].astype(jnp.float32) * scale

    return pl.pallas_call(
        kernel,
        grid=(2,),
        out_shape=jax.ShapeDtypeStruct((hid, CHUNKS * X * LANE), jnp.float32),
        in_specs=[pl.BlockSpec((X, CHUNKS, rows, LANE), lambda i: (0, 0, i, 0))],
        out_specs=pl.BlockSpec((rows, CHUNKS * X * LANE), lambda i: (i, 0)),
        name="finish",
    )(parts)


def per_device(heads, weight, cot):
    xi, yi = lax.axis_index("x"), lax.axis_index("y")
    zl, core, zh = lax.axis_index("zl"), lax.axis_index("core"), lax.axis_index("zh")
    tok, feat = cot.shape
    hid = weight.shape[0]
    blk = tok // ZH
    grad_scale = float(heads.shape[0] * ZH * Y * X) ** (-0.5)

    def order(m, c):
        return (m % ZL) * CORE + c

    rows = [[order(zl, c), order(zl + 2, c), order(zl + 1, c)] for c in (core, 1 - core)]

    cot2 = jnp.concatenate([cot, cot], axis=0)
    cot_sends = lax.dynamic_slice(cot2, (zh * blk, 0), (tok, feat))
    got = [
        lax.ppermute(cot_sends[k * blk:(k + 1) * blk], ("zl", "core", "zh"), spread_pairs(k)) for k in range(ZH)
    ]

    wr, wc = hid // Y, feat // X
    w_part = lax.dynamic_slice(weight, (yi * wr, xi * wc), (wr, wc))
    w_far = [lax.ppermute(w_part, "zh", ring(ZH, k)) for k in range(1, ZH)]
    w_y = spread_cols([w_part] + w_far, zh)
    w_y = lax.all_to_all(w_y, "y", 0, 0)
    w_y = weight_rows(w_y)
    w_x = [w_y] + [lax.ppermute(w_y, "x", ring(X, k)) for k in range(1, X)]

    heads_t = order_heads(heads, rows)

    mine = gather_tokens(got, (zh * ROW + zl * CORE + core) % ZH)
    near = []
    for h in range(CHUNKS):
        near.append([mine[h]] + [lax.ppermute(mine[h], "zl", ring(ZL, k)) for k in (1, 2)])
    parts, owns, oths = [], [], []
    for h in range(CHUNKS):
        own = jnp.concatenate(near[h], axis=0)
        oth = lax.ppermute(own, "core", ring(CORE, 1))
        owns.append(own)
        oths.append(oth)
        part = weight_part(heads_t, own, oth)
        parts.append(lax.all_to_all(part, "x", 0, 0))

    r = sum_split(parts)
    r = lax.all_to_all(r.reshape((Y * ZH,) + r.shape[2:]), ("y", "zh"), 0, 0)
    r = spread_sum(r)
    r = lax.all_to_all(r, "y", 0, 0)
    r = spread_rows(r)
    r = lax.all_to_all(r, "x", 0, 0)
    weight_grad = finish(r, grad_scale)

    head_grad = heads_grad(owns, oths, w_x, rows, xi)
    return head_grad, weight_grad


def solution(mesh):
    fine = Mesh(mesh.devices.reshape(Y, X, ZL, CORE, ZH), ("y", "x", "zl", "core", "zh"))

    return jax.shard_map(
        per_device,
        mesh=fine,
        in_specs=(P(("y", "x", "zh"), ("zl", "core")), P(("zl", "core"), "zh"), P(("y", "x", "zl", "core"), "zh")),
        out_specs=(P(("y", "x", "zh"), ("zl", "core")), P(("zl", "core"), "zh")),
        check_vma=False,
    )
```

profile of v0, /device:TPU:8, one launch (start us, length us, event | category | flops | bytes accessed | tf_op | source)
XLA Modules:
  0.0 322.8 jit_solution(468903292773877502)
XLA Ops:
  3.5 7.4 %collective-permute-start.1 = (bf16[128,1024]{1,0:T(8,128)(2,1)S(1)}, bf16[128,1024]{1,0:T(8,128)(2,1)S(1)}, u32[]{:S(2)}, u32[]{:S(2)}) collective-permute-start(bf16[128,1024]{1,0:T(8,128)(2,1)S(1)} %get-tuple-element.12), channel_id=1, source_target_pairs={{0,4},{1,8},{2,12},{3,0},{4,20},{5,1},{6,5},{7,16},{8,13},{9,17},{... | collective-permute-start | bytes 786440 | tf_op jit(solution)/shard_map/ppermute | solution.py:268
  10.9 10.5 %collective-permute-start.2 = (bf16[128,1024]{1,0:T(8,128)(2,1)S(1)}, bf16[128,1024]{1,0:T(8,128)(2,1)S(1)}, u32[]{:S(2)}, u32[]{:S(2)}) collective-permute-start(bf16[128,1024]{1,0:T(8,128)(2,1)S(1)} %get-tuple-element.11), channel_id=1, source_target_pairs={{0,8},{1,12},{2,0},{3,4},{4,1},{5,5},{6,16},{7,20},{8,17},{9,21},{... | collective-permute-start | bytes 786440 | tf_op jit(solution)/shard_map/ppermute | solution.py:268
  21.4 8.3 %collective-permute-start.3 = (bf16[128,1024]{1,0:T(8,128)(2,1)S(1)}, bf16[128,1024]{1,0:T(8,128)(2,1)S(1)}, u32[]{:S(2)}, u32[]{:S(2)}) collective-permute-start(bf16[128,1024]{1,0:T(8,128)(2,1)S(1)} %get-tuple-element.10), channel_id=1, source_target_pairs={{0,12},{1,0},{2,4},{3,8},{4,5},{5,16},{6,20},{7,1},{8,21},{9,9},{1... | collective-permute-start | bytes 786440 | tf_op jit(solution)/shard_map/ppermute | solution.py:268
  29.7 16.8 %collective-permute-done.2.refs_2_ = bf16[128,1024]{1,0:T(8,128)(2,1)S(1)} collective-permute-done((bf16[128,1024]{1,0:T(8,128)(2,1)S(1)}, bf16[128,1024]{1,0:T(8,128)(2,1)S(1)}, u32[]{:S(2)}, u32[]{:S(2)}) %collective-permute-start.2) | collective-permute-done | bytes 262176 | tf_op jit(solution)/shard_map/ppermute | solution.py:268
  49.8 14.5 %collective-permute-start.4 = (bf16[128,2048]{1,0:T(8,128)(2,1)}, bf16[128,2048]{1,0:T(8,128)(2,1)S(1)}, u32[]{:S(2)}, u32[]{:S(2)}) collective-permute-start(bf16[128,2048]{1,0:T(8,128)(2,1)} %get-tuple-element.6), channel_id=1, source_target_pairs={{0,8},{8,16},{16,0},{1,9},{9,17},{17,1},{2,10},{10,18},{18,2},{3,1... | collective-permute-start | bytes 1572872 | tf_op jit(solution)/shard_map/ppermute | solution.py:284
  67.4 9.1 %collective-permute-done.4 = bf16[128,2048]{1,0:T(8,128)(2,1)S(1)} collective-permute-done((bf16[128,2048]{1,0:T(8,128)(2,1)}, bf16[128,2048]{1,0:T(8,128)(2,1)S(1)}, u32[]{:S(2)}, u32[]{:S(2)}) %collective-permute-start.4) | collective-permute-done | bytes 524320 | tf_op jit(solution)/shard_map/ppermute | solution.py:284
  76.5 11.2 %collective-permute-done.5 = bf16[128,2048]{1,0:T(8,128)(2,1)S(1)} collective-permute-done((bf16[128,2048]{1,0:T(8,128)(2,1)}, bf16[128,2048]{1,0:T(8,128)(2,1)S(1)}, u32[]{:S(2)}, u32[]{:S(2)}) %collective-permute-start.5) | collective-permute-done | bytes 524320 | tf_op jit(solution)/shard_map/ppermute | solution.py:284
  92.2 4.9 %collective-permute-start.7 = (bf16[128,2048]{1,0:T(8,128)(2,1)S(1)}, bf16[128,2048]{1,0:T(8,128)(2,1)S(1)}, u32[]{:S(2)}, u32[]{:S(2)}) collective-permute-start(bf16[128,2048]{1,0:T(8,128)(2,1)S(1)} %copy-done.10), channel_id=1, source_target_pairs={{0,16},{8,0},{16,8},{1,17},{9,1},{17,9},{2,18},{10,2},{18,10},{3,1... | collective-permute-start | bytes 1572872 | tf_op jit(solution)/shard_map/ppermute | solution.py:284
  97.2 10.8 %collective-permute-done.6 = bf16[128,2048]{1,0:T(8,128)(2,1)S(1)} collective-permute-done((bf16[128,2048]{1,0:T(8,128)(2,1)S(1)}, bf16[128,2048]{1,0:T(8,128)(2,1)S(1)}, u32[]{:S(2)}, u32[]{:S(2)}) %collective-permute-start.6) | collective-permute-done | bytes 524320 | tf_op jit(solution)/shard_map/ppermute | solution.py:284
  108.0 10.7 %collective-permute-done.7 = bf16[128,2048]{1,0:T(8,128)(2,1)S(1)} collective-permute-done((bf16[128,2048]{1,0:T(8,128)(2,1)S(1)}, bf16[128,2048]{1,0:T(8,128)(2,1)S(1)}, u32[]{:S(2)}, u32[]{:S(2)}) %collective-permute-start.7) | collective-permute-done | bytes 524320 | tf_op jit(solution)/shard_map/ppermute | solution.py:284
  123.5 5.2 %weight_part.2 = bf16[4,384,512]{2,1,0:T(8,128)(2,1)} custom-call(bf16[384,384]{1,0:T(8,128)(2,1)} %get-tuple-element.8.a, bf16[384,384]{1,0:T(8,128)(2,1)} %get-tuple-element.9.b, bf16[384,2048]{1,0:T(8,128)(2,1)} %copy-done, bf16[384,2048]{1,0:T(8,128)(2,1)} %collective-permute-done.8.refs_2_.d), custom_call_target="tpu_custom_call" | custom-call | tf_op jit(solution)/shard_map/weight_part/pallas_call | solution.py:131
  132.9 5.2 %weight_part.3 = bf16[4,384,512]{2,1,0:T(8,128)(2,1)} custom-call(bf16[384,384]{1,0:T(8,128)(2,1)} %get-tuple-element.8.a, bf16[384,384]{1,0:T(8,128)(2,1)} %get-tuple-element.9.b, bf16[384,2048]{1,0:T(8,128)(2,1)} %copy-done.1, bf16[384,2048]{1,0:T(8,128)(2,1)} %collective-permute-done.9.refs_3_.d), custom_call_target="tpu_custom_call" | custom-call | tf_op jit(solution)/shard_map/weight_part/pallas_call | solution.py:131
  138.1 16.2 %all-to-all-done.1.refs_0_ = bf16[4,384,512]{2,1,0:T(8,128)(2,1)S(1)} async-done(((bf16[4,384,512]{2,1,0:T(8,128)(2,1)}), bf16[4,384,512]{2,1,0:T(8,128)(2,1)S(1)}, u32[]{:S(2)}, u32[]{:S(2)}) %all-to-all-start.1) | async-done | bytes 1572896 | tf_op jit(solution)/shard_map/all_to_all | solution.py:292
  154.3 24.9 %all_to_all.30.refs_1_ = bf16[4,384,512]{2,1,0:T(8,128)(2,1)} all-to-all(bf16[4,384,512]{2,1,0:T(8,128)(2,1)} %weight_part.3), channel_id=1, replica_groups=mesh['y'=8,'x'=4,'zl'=3,'core'=2,'zh'=4] {'x'}, dimensions={0} | all-to-all | bytes 3145728 | tf_op jit(solution)/shard_map/all_to_all | solution.py:292
  179.2 5.8 %sum_split.1 = bf16[8,4,2,48,128]{4,3,2,1,0:T(8,128)(2,1)} custom-call(bf16[4,384,512]{2,1,0:T(8,128)(2,1)} %copy-done.2, bf16[4,384,512]{2,1,0:T(8,128)(2,1)} %all_to_all.30.refs_1_), custom_call_target="tpu_custom_call" | custom-call | tf_op jit(solution)/shard_map/sum_split/pallas_call | solution.py:187
  185.0 11.6 %all-to-all-start.3 = ((bf16[32,2,48,128]{3,2,1,0:T(8,128)(2,1)}), bf16[32,2,48,128]{3,2,1,0:T(8,128)(2,1)S(1)}, u32[]{:S(2)}, u32[]{:S(2)}) async-start(bf16[32,2,48,128]{3,2,1,0:T(8,128)(2,1)} %bitcast.10), calls=%async_computation.3 | async-start | bytes 1572864 | tf_op jit(solution)/shard_map/all_to_all | solution.py:295
  197.4 5.2 %collective-permute-start.10 = (bf16[48,256]{1,0:T(8,128)(2,1)S(1)}, bf16[48,256]{1,0:T(8,128)(2,1)S(1)}, u32[]{:S(2)}, u32[]{:S(2)}) collective-permute-start(bf16[48,256]{1,0:T(8,128)(2,1)S(1)} %dynamic_slice.7.refs_0_), channel_id=1, source_target_pairs={{0,1},{1,2},{2,3},{3,0},{4,5},{5,6},{6,7},{7,4},{8,9},{9,10},{10,1... | collective-permute-start | bytes 73736 | tf_op jit(solution)/shard_map/ppermute | solution.py:273
  202.5 7.6 %collective-permute-start.11 = (bf16[48,256]{1,0:T(8,128)(2,1)S(1)}, bf16[48,256]{1,0:T(8,128)(2,1)S(1)}, u32[]{:S(2)}, u32[]{:S(2)}) collective-permute-start(bf16[48,256]{1,0:T(8,128)(2,1)S(1)} %dynamic_slice.7.refs_0_), channel_id=1, source_target_pairs={{0,2},{1,3},{2,0},{3,1},{4,6},{5,7},{6,4},{7,5},{8,10},{9,11},{10,... | collective-permute-start | bytes 73736 | tf_op jit(solution)/shard_map/ppermute | solution.py:273
  210.1 5.2 %collective-permute-start.12 = (bf16[48,256]{1,0:T(8,128)(2,1)S(1)}, bf16[48,256]{1,0:T(8,128)(2,1)S(1)}, u32[]{:S(2)}, u32[]{:S(2)}) collective-permute-start(bf16[48,256]{1,0:T(8,128)(2,1)S(1)} %dynamic_slice.7.refs_0_), channel_id=1, source_target_pairs={{0,3},{1,0},{2,1},{3,2},{4,7},{5,4},{6,5},{7,6},{8,11},{9,8},{10,9... | collective-permute-start | bytes 73736 | tf_op jit(solution)/shard_map/ppermute | solution.py:273
  215.3 12.1 %collective-permute-done.10.refs_1_ = bf16[48,256]{1,0:T(8,128)(2,1)S(1)} collective-permute-done((bf16[48,256]{1,0:T(8,128)(2,1)S(1)}, bf16[48,256]{1,0:T(8,128)(2,1)S(1)}, u32[]{:S(2)}, u32[]{:S(2)}) %collective-permute-start.10) | collective-permute-done | bytes 24608 | tf_op jit(solution)/shard_map/ppermute | solution.py:273
  231.6 7.0 %all-to-all-start = ((bf16[8,4,48,256]{3,2,1,0:T(8,128)(2,1)}), bf16[8,4,48,256]{3,2,1,0:T(8,128)(2,1)S(1)}, u32[]{:S(2)}, u32[]{:S(2)}) async-start(bf16[8,4,48,256]{3,2,1,0:T(8,128)(2,1)} %spread_cols.1), calls=%async_computation | async-start | bytes 1572864 | tf_op jit(solution)/shard_map/all_to_all | solution.py:275
  240.5 18.3 %all-to-all-done.src = bf16[8,4,48,256]{3,2,1,0:T(8,128)(2,1)S(1)} async-done(((bf16[8,4,48,256]{3,2,1,0:T(8,128)(2,1)}), bf16[8,4,48,256]{3,2,1,0:T(8,128)(2,1)S(1)}, u32[]{:S(2)}, u32[]{:S(2)}) %all-to-all-start) | async-done | bytes 786464 | tf_op jit(solution)/shard_map/all_to_all | solution.py:275
  281.5 25.3 %collective-permute-done.13.refs_5_ = bf16[384,1024]{1,0:T(8,128)(2,1)S(1)} collective-permute-done((bf16[384,1024]{1,0:T(8,128)(2,1)}, bf16[384,1024]{1,0:T(8,128)(2,1)S(1)}, u32[]{:S(2)}, u32[]{:S(2)}) %collective-permute-start.13) | collective-permute-done | bytes 786464 | tf_op jit(solution)/shard_map/ppermute | solution.py:277
  310.0 9.6 %heads_grad.1 = bf16[768,384]{1,0:T(8,128)(2,1)} custom-call(s32[1]{0:T(128)} %bitcast.at_ref, s32[6]{0:T(128)} %stack.34.rows_ref, bf16[384,2048]{1,0:T(8,128)(2,1)} %copy-done, bf16[384,2048]{1,0:T(8,128)(2,1)} %copy-done.1, bf16[384,2048]{1,0:T(8,128)(2,1)} %collective-permute-done.8.refs_2_.d, bf16[384,2048]{1,0:T(8,128)(2,1)} %collective-permute-done.9.refs_3_.d, ...), custom_call_target="tpu_custom_call" | custom-call | tf_op jit(solution)/shard_map/heads_grad/pallas_call | solution.py:167
  (78 shorter events, 58.4 us)
Async XLA Ops:
  2.8 26.9 %collective-permute-start = (bf16[128,1024]{1,0:T(8,128)(2,1)S(1)}, bf16[128,1024]{1,0:T(8,128)(2,1)S(1)}, u32[]{:S(2)}, u32[]{:S(2)}) collective-permute-start(bf16[128,1024]{1,0:T(8,128)(2,1)S(1)} %get-tuple-element.13), channel_id=1, source_target_pairs={{0,0},{1,4},{2,8},{3,12},{4,16},{5,20},{6,1},{7,5},{8,9},{9,13},{1... | collective-permute-start | bytes 786440 | tf_op jit(solution)/shard_map/ppermute | solution.py:268
  3.5 26.3 %collective-permute-start.1 = (bf16[128,1024]{1,0:T(8,128)(2,1)S(1)}, bf16[128,1024]{1,0:T(8,128)(2,1)S(1)}, u32[]{:S(2)}, u32[]{:S(2)}) collective-permute-start(bf16[128,1024]{1,0:T(8,128)(2,1)S(1)} %get-tuple-element.12), channel_id=1, source_target_pairs={{0,4},{1,8},{2,12},{3,0},{4,20},{5,1},{6,5},{7,16},{8,13},{9,17},{... | collective-permute-start | bytes 786440 | tf_op jit(solution)/shard_map/ppermute | solution.py:268
  10.9 35.6 %collective-permute-start.2 = (bf16[128,1024]{1,0:T(8,128)(2,1)S(1)}, bf16[128,1024]{1,0:T(8,128)(2,1)S(1)}, u32[]{:S(2)}, u32[]{:S(2)}) collective-permute-start(bf16[128,1024]{1,0:T(8,128)(2,1)S(1)} %get-tuple-element.11), channel_id=1, source_target_pairs={{0,8},{1,12},{2,0},{3,4},{4,1},{5,5},{6,16},{7,20},{8,17},{9,21},{... | collective-permute-start | bytes 786440 | tf_op jit(solution)/shard_map/ppermute | solution.py:268
  21.4 25.1 %collective-permute-start.3 = (bf16[128,1024]{1,0:T(8,128)(2,1)S(1)}, bf16[128,1024]{1,0:T(8,128)(2,1)S(1)}, u32[]{:S(2)}, u32[]{:S(2)}) collective-permute-start(bf16[128,1024]{1,0:T(8,128)(2,1)S(1)} %get-tuple-element.10), channel_id=1, source_target_pairs={{0,12},{1,0},{2,4},{3,8},{4,5},{5,16},{6,20},{7,1},{8,21},{9,9},{1... | collective-permute-start | bytes 786440 | tf_op jit(solution)/shard_map/ppermute | solution.py:268
  49.8 40.5 %copy-start.10 = (bf16[128,2048]{1,0:T(8,128)(2,1)S(1)}, bf16[128,2048]{1,0:T(8,128)(2,1)}, u32[]{:S(2)}) copy-start(bf16[128,2048]{1,0:T(8,128)(2,1)} %get-tuple-element.7) | copy-start | bytes 1572868
  49.8 26.7 %collective-permute-start.4 = (bf16[128,2048]{1,0:T(8,128)(2,1)}, bf16[128,2048]{1,0:T(8,128)(2,1)S(1)}, u32[]{:S(2)}, u32[]{:S(2)}) collective-permute-start(bf16[128,2048]{1,0:T(8,128)(2,1)} %get-tuple-element.6), channel_id=1, source_target_pairs={{0,8},{8,16},{16,0},{1,9},{9,17},{17,1},{2,10},{10,18},{18,2},{3,1... | collective-permute-start | bytes 1572872 | tf_op jit(solution)/shard_map/ppermute | solution.py:284
  64.3 23.4 %collective-permute-start.5 = (bf16[128,2048]{1,0:T(8,128)(2,1)}, bf16[128,2048]{1,0:T(8,128)(2,1)S(1)}, u32[]{:S(2)}, u32[]{:S(2)}) collective-permute-start(bf16[128,2048]{1,0:T(8,128)(2,1)} %get-tuple-element.6), channel_id=1, source_target_pairs={{0,16},{8,0},{16,8},{1,17},{9,1},{17,9},{2,18},{10,2},{18,10},{3,1... | collective-permute-start | bytes 1572872 | tf_op jit(solution)/shard_map/ppermute | solution.py:284
  87.8 31.0 %copy-start = (bf16[384,2048]{1,0:T(8,128)(2,1)}, bf16[384,2048]{1,0:T(8,128)(2,1)S(1)}, u32[]{:S(2)}) copy-start(bf16[384,2048]{1,0:T(8,128)(2,1)S(1)} %constant_dynamic-update-slice_fusion.refs_0_.c) | copy-start | bytes 4718596
  87.8 35.7 %collective-permute-start.8 = (bf16[384,2048]{1,0:T(8,128)(2,1)S(1)}, bf16[384,2048]{1,0:T(8,128)(2,1)}, u32[]{:S(2)}, u32[]{:S(2)}) collective-permute-start(bf16[384,2048]{1,0:T(8,128)(2,1)S(1)} %constant_dynamic-update-slice_fusion.refs_0_.c), channel_id=1, source_target_pairs={{0,4},{4,0},{1,5},{5,1},{2,6},{6,2},{3,7},{7,3},{8,12},{12,8},{9,1... | collective-permute-start | bytes 4718600 | tf_op jit(solution)/shard_map/ppermute | solution.py:288
  90.3 17.7 %collective-permute-start.6 = (bf16[128,2048]{1,0:T(8,128)(2,1)S(1)}, bf16[128,2048]{1,0:T(8,128)(2,1)S(1)}, u32[]{:S(2)}, u32[]{:S(2)}) collective-permute-start(bf16[128,2048]{1,0:T(8,128)(2,1)S(1)} %copy-done.10), channel_id=1, source_target_pairs={{0,8},{8,16},{16,0},{1,9},{9,17},{17,1},{2,10},{10,18},{18,2},{3,1... | collective-permute-start | bytes 1572872 | tf_op jit(solution)/shard_map/ppermute | solution.py:284
  92.2 26.5 %collective-permute-start.7 = (bf16[128,2048]{1,0:T(8,128)(2,1)S(1)}, bf16[128,2048]{1,0:T(8,128)(2,1)S(1)}, u32[]{:S(2)}, u32[]{:S(2)}) collective-permute-start(bf16[128,2048]{1,0:T(8,128)(2,1)S(1)} %copy-done.10), channel_id=1, source_target_pairs={{0,16},{8,0},{16,8},{1,17},{9,1},{17,9},{2,18},{10,2},{18,10},{3,1... | collective-permute-start | bytes 1572872 | tf_op jit(solution)/shard_map/ppermute | solution.py:284
  118.8 14.2 %collective-permute-start.9 = (bf16[384,2048]{1,0:T(8,128)(2,1)S(1)}, bf16[384,2048]{1,0:T(8,128)(2,1)}, u32[]{:S(2)}, u32[]{:S(2)}) collective-permute-start(bf16[384,2048]{1,0:T(8,128)(2,1)S(1)} %constant_dynamic-update-slice_fusion.3.refs_1_.c), channel_id=1, source_target_pairs={{0,4},{4,0},{1,5},{5,1},{2,6},{6,2},{3,7},{7,3},{8,12},{12,8},{9,1... | collective-permute-start | bytes 4718600 | tf_op jit(solution)/shard_map/ppermute | solution.py:288
  128.6 25.6 %all-to-all-start.1 = ((bf16[4,384,512]{2,1,0:T(8,128)(2,1)}), bf16[4,384,512]{2,1,0:T(8,128)(2,1)S(1)}, u32[]{:S(2)}, u32[]{:S(2)}) async-start(bf16[4,384,512]{2,1,0:T(8,128)(2,1)} %weight_part.2), calls=%async_computation.1 | async-start | bytes 3145728 | tf_op jit(solution)/shard_map/all_to_all | solution.py:292
  185.0 46.6 %all-to-all-start.3 = ((bf16[32,2,48,128]{3,2,1,0:T(8,128)(2,1)}), bf16[32,2,48,128]{3,2,1,0:T(8,128)(2,1)S(1)}, u32[]{:S(2)}, u32[]{:S(2)}) async-start(bf16[32,2,48,128]{3,2,1,0:T(8,128)(2,1)} %bitcast.10), calls=%async_computation.3 | async-start | bytes 1572864 | tf_op jit(solution)/shard_map/all_to_all | solution.py:295
  197.3 31.6 %copy-start.15 = (bf16[48,256]{1,0:T(8,128)(2,1)}, bf16[48,256]{1,0:T(8,128)(2,1)S(1)}, u32[]{:S(2)}) copy-start(bf16[48,256]{1,0:T(8,128)(2,1)S(1)} %dynamic_slice.7.refs_0_) | copy-start | bytes 73732
  197.4 30.1 %collective-permute-start.10 = (bf16[48,256]{1,0:T(8,128)(2,1)S(1)}, bf16[48,256]{1,0:T(8,128)(2,1)S(1)}, u32[]{:S(2)}, u32[]{:S(2)}) collective-permute-start(bf16[48,256]{1,0:T(8,128)(2,1)S(1)} %dynamic_slice.7.refs_0_), channel_id=1, source_target_pairs={{0,1},{1,2},{2,3},{3,0},{4,5},{5,6},{6,7},{7,4},{8,9},{9,10},{10,1... | collective-permute-start | bytes 73736 | tf_op jit(solution)/shard_map/ppermute | solution.py:273
  202.5 26.4 %collective-permute-start.11 = (bf16[48,256]{1,0:T(8,128)(2,1)S(1)}, bf16[48,256]{1,0:T(8,128)(2,1)S(1)}, u32[]{:S(2)}, u32[]{:S(2)}) collective-permute-start(bf16[48,256]{1,0:T(8,128)(2,1)S(1)} %dynamic_slice.7.refs_0_), channel_id=1, source_target_pairs={{0,2},{1,3},{2,0},{3,1},{4,6},{5,7},{6,4},{7,5},{8,10},{9,11},{10,... | collective-permute-start | bytes 73736 | tf_op jit(solution)/shard_map/ppermute | solution.py:273
  210.1 18.8 %collective-permute-start.12 = (bf16[48,256]{1,0:T(8,128)(2,1)S(1)}, bf16[48,256]{1,0:T(8,128)(2,1)S(1)}, u32[]{:S(2)}, u32[]{:S(2)}) collective-permute-start(bf16[48,256]{1,0:T(8,128)(2,1)S(1)} %dynamic_slice.7.refs_0_), channel_id=1, source_target_pairs={{0,3},{1,0},{2,1},{3,2},{4,7},{5,4},{6,5},{7,6},{8,11},{9,8},{10,9... | collective-permute-start | bytes 73736 | tf_op jit(solution)/shard_map/ppermute | solution.py:273
  231.6 27.2 %all-to-all-start = ((bf16[8,4,48,256]{3,2,1,0:T(8,128)(2,1)}), bf16[8,4,48,256]{3,2,1,0:T(8,128)(2,1)S(1)}, u32[]{:S(2)}, u32[]{:S(2)}) async-start(bf16[8,4,48,256]{3,2,1,0:T(8,128)(2,1)} %spread_cols.1), calls=%async_computation | async-start | bytes 1572864 | tf_op jit(solution)/shard_map/all_to_all | solution.py:275
  258.8 15.9 %all-to-all-start.4 = ((bf16[8,2,48,128]{3,2,1,0:T(8,128)(2,1)}), bf16[8,2,48,128]{3,2,1,0:T(8,128)(2,1)S(1)}, u32[]{:S(2)}, u32[]{:S(2)}) async-start(bf16[8,2,48,128]{3,2,1,0:T(8,128)(2,1)} %spread_sum.1), calls=%async_computation.4 | async-start | bytes 393216 | tf_op jit(solution)/shard_map/all_to_all | solution.py:297
  265.7 41.1 %collective-permute-start.13 = (bf16[384,1024]{1,0:T(8,128)(2,1)}, bf16[384,1024]{1,0:T(8,128)(2,1)S(1)}, u32[]{:S(2)}, u32[]{:S(2)}) collective-permute-start(bf16[384,1024]{1,0:T(8,128)(2,1)} %weight_rows.1.refs_4_), channel_id=1, source_target_pairs={{0,24},{24,48},{48,72},{72,0},{1,25},{25,49},{49,73},{73,1},{2,26}... | collective-permute-start | bytes 2359304 | tf_op jit(solution)/shard_map/ppermute | solution.py:277
  268.2 38.7 %collective-permute-start.14 = (bf16[384,1024]{1,0:T(8,128)(2,1)}, bf16[384,1024]{1,0:T(8,128)(2,1)S(1)}, u32[]{:S(2)}, u32[]{:S(2)}) collective-permute-start(bf16[384,1024]{1,0:T(8,128)(2,1)} %weight_rows.1.refs_4_), channel_id=1, source_target_pairs={{0,48},{24,72},{48,0},{72,24},{1,49},{25,73},{49,1},{73,25},{2,50}... | collective-permute-start | bytes 2359304 | tf_op jit(solution)/shard_map/ppermute | solution.py:277
  272.2 36.9 %collective-permute-start.15 = (bf16[384,1024]{1,0:T(8,128)(2,1)}, bf16[384,1024]{1,0:T(8,128)(2,1)S(1)}, u32[]{:S(2)}, u32[]{:S(2)}) collective-permute-start(bf16[384,1024]{1,0:T(8,128)(2,1)} %weight_rows.1.refs_4_), channel_id=1, source_target_pairs={{0,72},{24,0},{48,24},{72,48},{1,73},{25,1},{49,25},{73,49},{2,74}... | collective-permute-start | bytes 2359304 | tf_op jit(solution)/shard_map/ppermute | solution.py:277
  277.3 42.3 %all-to-all-start.5 = ((bf16[4,2,384,128]{3,2,1,0:T(8,128)(2,1)}), bf16[4,2,384,128]{3,2,1,0:T(8,128)(2,1)S(1)}, u32[]{:S(2)}, u32[]{:S(2)}) async-start(bf16[4,2,384,128]{3,2,1,0:T(8,128)(2,1)} %spread_rows.1), calls=%async_computation.5 | async-start | bytes 1572864 | tf_op jit(solution)/shard_map/all_to_all | solution.py:299
  (16 other events, 91.5 us)
where the time goes:
time: 324 us; the launch traced here: 323 us
  waiting for transfers between devices  134 us (41%)
  starting transfers between devices  113 us (35%)
  Pallas kernels  40.3 us (12%)
  blocking collectives  24.9 us (8%)
  local copies, waits for them, and re-layouts  6.69 us (2%)
    ppermute x4, waiting for transfers between devices, per_device(): lax.ppermute(mine[h], 'zl', ring(ZL, k))  41.8 us
    ppermute x3, waiting for transfers between devices, per_device(): w_x = [w_y] + [lax.ppermute(w_y, 'x', ring(X, k)) for k in range(1, X)]  27.5 us
    ppermute x4, starting transfers between devices, per_device(): lax.ppermute(cot_sends[k * blk:(k + 1) * blk], ('zl', 'core', 'zh'), spre...  26.9 us
    all_to_all x1, blocking collectives, per_device(): parts.append(lax.all_to_all(part, 'x', 0, 0))  24.9 us
    ppermute x4, starting transfers between devices, per_device(): lax.ppermute(mine[h], 'zl', ring(ZL, k))  23.3 us
    all_to_all x1, waiting for transfers between devices, per_device(): w_y = lax.all_to_all(w_y, 'y', 0, 0)  18.3 us
    ppermute x3, starting transfers between devices, per_device(): w_far = [lax.ppermute(w_part, 'zh', ring(ZH, k)) for k in range(1, ZH)]  17.9 us
    ppermute x4, waiting for transfers between devices, per_device(): lax.ppermute(cot_sends[k * blk:(k + 1) * blk], ('zl', 'core', 'zh'), spre...  16.8 us
  transfers between devices with their start and end apart: 21, of which 12 were waited for; matrix products, arithmetic and copies ran while one was open for 1% of the time, Pallas kernels for 9%

commit v1 on v0

--- a/solution.py
+++ b/solution.py
@@ -119,23 +119,24 @@
     )(pieces)
 
 
-def weight_part(heads_t, own, oth):
-    hid, half = heads_t[0].shape
+def weight_part(heads_t, own, oth, at):
+    hid = heads_t[0].shape[0]
     n = ZH * LANE
 
-    def kernel(a, b, c, d, out):
-        acc = jnp.dot(a[...], c[...], preferred_element_type=jnp.float32)
-        acc += jnp.dot(b[...], d[...], preferred_element_type=jnp.float32)
-        out[0] = acc.astype(out.dtype)
-
-    return pl.pallas_call(
-        kernel,
-        grid=(XS,),
-        out_shape=jax.ShapeDtypeStruct((XS, hid, n), own.dtype),
-        in_specs=[pl.BlockSpec((hid, half), lambda s: (0, 0))] * 2 + [pl.BlockSpec((half, n), lambda s: (0, s))] * 2,
-        out_specs=pl.BlockSpec((1, hid, n), lambda s: (s, 0, 0)),
+    def kernel(at_ref, a, b, c, d, *outs):
+        for k in range(X):
+            lo = pl.multiple_of((at_ref[0] + k) % X * n, n)
+            acc = jnp.dot(a[...], c[:, pl.ds(lo, n)], preferred_element_type=jnp.float32)
+            acc += jnp.dot(b[...], d[:, pl.ds(lo, n)], preferred_element_type=jnp.float32)
+            outs[k][...] = acc.astype(own.dtype)
+
+    return pl.pallas_call(
+        kernel,
+        out_shape=[jax.ShapeDtypeStruct((hid, n), own.dtype)] * X,
+        in_specs=[SMEM] + [VMEM] * 4,
+        out_specs=[VMEM] * X,
         name="weight_part",
-    )(*heads_t, own, oth)
+    )(at.reshape(1), *heads_t, own, oth)
 
 
 def heads_grad(owns, oths, weights, rows, at):
@@ -175,40 +176,45 @@
 
 
 def sum_split(parts):
-    rows = parts[0].shape[1] // Y
+    hid = parts[0].shape[0]
+    rows = hid // Y
+
+    def kernel(*refs):
+        out = refs[-1]
+        for y in range(Y):
+            for col in range(ZH):
+                total = None
+                for ref in refs[:-1]:
+                    v = ref[y * rows:(y + 1) * rows, col * LANE:(col + 1) * LANE].astype(jnp.float32)
+                    total = v if total is None else total + v
+                out[y, col] = total.astype(out.dtype)
+
+    return pl.pallas_call(
+        kernel,
+        out_shape=jax.ShapeDtypeStruct((Y, ZH, rows, LANE), parts[0].dtype),
+        in_specs=[VMEM] * len(parts),
+        out_specs=VMEM,
+        name="sum_split",
+    )(*parts)
+
+
+def spread_sum(parts):
+    shape = (Y, CHUNKS) + parts[0].shape[1:]
 
     def kernel(*refs):
         out = refs[-1]
         for h in range(CHUNKS):
-            for col in range(ZH):
-                v = refs[h][:, :, col * LANE:(col + 1) * LANE].astype(jnp.float32)
-                out[0, col, h] = jnp.sum(v, axis=0).astype(out.dtype)
-
-    return pl.pallas_call(
-        kernel,
-        grid=(Y,),
-        out_shape=jax.ShapeDtypeStruct((Y, ZH, CHUNKS, rows, LANE), parts[0].dtype),
-        in_specs=[pl.BlockSpec((X, rows, ZH * LANE), lambda y: (0, y, 0))] * CHUNKS,
-        out_specs=pl.BlockSpec((1, ZH, CHUNKS, rows, LANE), lambda y: (y, 0, 0, 0, 0)),
-        name="sum_split",
+            total = jnp.sum(refs[h][...].astype(jnp.float32), axis=0).astype(out.dtype)
+            for y in range(Y):
+                out[y, h] = total
+
+    return pl.pallas_call(
+        kernel,
+        out_shape=jax.ShapeDtypeStruct(shape, parts[0].dtype),
+        in_specs=[VMEM] * CHUNKS,
+        out_specs=VMEM,
+        name="spread_sum",
     )(*parts)
-
-
-def spread_sum(parts):
-    shape = parts.shape[1:]
-
-    def kernel(src, out):
-        total = jnp.sum(src[...].astype(jnp.float32), axis=0).astype(out.dtype)
-        for y in range(Y):
-            out[y] = total
-
-    return pl.pallas_call(
-        kernel,
-        out_shape=jax.ShapeDtypeStruct((Y,) + shape, parts.dtype),
-        in_specs=[VMEM],
-        out_specs=VMEM,
-        name="spread_sum",
-    )(parts)
 
 
 def spread_rows(parts):
@@ -288,12 +294,13 @@
         oth = lax.ppermute(own, "core", ring(CORE, 1))
         owns.append(own)
         oths.append(oth)
-        part = weight_part(heads_t, own, oth)
-        parts.append(lax.all_to_all(part, "x", 0, 0))
-
-    r = sum_split(parts)
-    r = lax.all_to_all(r.reshape((Y * ZH,) + r.shape[2:]), ("y", "zh"), 0, 0)
-    r = spread_sum(r)
+        part = weight_part(heads_t, own, oth, xi)
+        parts.append([part[0]] + [lax.ppermute(part[k], "x", ring(X, k)) for k in range(1, X)])
+    sums = []
+    for h in range(CHUNKS):
+        r = sum_split(parts[h])
+        sums.append(lax.all_to_all(r.reshape((Y * ZH,) + r.shape[2:]), ("y", "zh"), 0, 0))
+    r = spread_sum(sums)
     r = lax.all_to_all(r, "y", 0, 0)
     r = spread_rows(r)
     r = lax.all_to_all(r, "x", 0, 0)

time: 324 us -> 332 us (1.025)
  the two profiles are of different devices: /device:TPU:8 before, /device:TPU:76 now
where the time goes in v1:
time: 332 us; the launch traced here: 331 us
  waiting for transfers between devices  148 us (45%)
  starting transfers between devices  134 us (40%)
  Pallas kernels  38 us (11%)
  local copies, waits for them, and re-layouts  8.12 us (2%)
    ppermute x4, waiting for transfers between devices, per_device(): lax.ppermute(mine[h], 'zl', ring(ZL, k))  38 us
    ppermute x6, waiting for transfers between devices, per_device(): lax.ppermute(part[k], 'x', ring(X, k))  32.5 us
    ppermute x4, waiting for transfers between devices, per_device(): lax.ppermute(cot_sends[k * blk:(k + 1) * blk], ('zl', 'core', 'zh'), spre...  29.8 us
    all_to_all x2, starting transfers between devices, per_device(): lax.all_to_all(r.reshape((Y * ZH,) + r.shape[2:]), ('y', 'zh'), 0, 0)  25.6 us
    ppermute x3, waiting for transfers between devices, per_device(): w_x = [w_y] + [lax.ppermute(w_y, 'x', ring(X, k)) for k in range(1, X)]  25.4 us
    ppermute x4, starting transfers between devices, per_device(): lax.ppermute(cot_sends[k * blk:(k + 1) * blk], ('zl', 'core', 'zh'), spre...  24.2 us
    all_to_all x1, waiting for transfers between devices, per_device(): w_y = lax.all_to_all(w_y, 'y', 0, 0)  19.1 us
    ppermute x3, starting transfers between devices, per_device(): w_far = [lax.ppermute(w_part, 'zh', ring(ZH, k)) for k in range(1, ZH)]  17.9 us
  transfers between devices with their start and end apart: 27, of which 20 were waited for; matrix products, arithmetic and copies ran while one was open for 1% of the time, Pallas kernels for 10%

profile of v1, /device:TPU:76, one launch (start us, length us, event | category | flops | bytes accessed | tf_op | source)
XLA Modules:
  0.0 330.7 jit_solution(8411575821305776463)
XLA Ops:
  2.8 9.1 %collective-permute-start = (bf16[128,1024]{1,0:T(8,128)(2,1)S(1)}, bf16[128,1024]{1,0:T(8,128)(2,1)S(1)}, u32[]{:S(2)}, u32[]{:S(2)}) collective-permute-start(bf16[128,1024]{1,0:T(8,128)(2,1)S(1)} %get-tuple-element.29), channel_id=1, source_target_pairs={{0,0},{1,4},{2,8},{3,12},{4,16},{5,20},{6,1},{7,5},{8,9},{9,13},{1... | collective-permute-start | bytes 786440 | tf_op jit(solution)/shard_map/ppermute | solution.py:274
  11.8 5.3 %collective-permute-start.1 = (bf16[128,1024]{1,0:T(8,128)(2,1)S(1)}, bf16[128,1024]{1,0:T(8,128)(2,1)S(1)}, u32[]{:S(2)}, u32[]{:S(2)}) collective-permute-start(bf16[128,1024]{1,0:T(8,128)(2,1)S(1)} %get-tuple-element.28), channel_id=1, source_target_pairs={{0,4},{1,8},{2,12},{3,0},{4,20},{5,1},{6,5},{7,16},{8,13},{9,17},{... | collective-permute-start | bytes 786440 | tf_op jit(solution)/shard_map/ppermute | solution.py:274
  17.1 6.1 %collective-permute-start.2 = (bf16[128,1024]{1,0:T(8,128)(2,1)S(1)}, bf16[128,1024]{1,0:T(8,128)(2,1)S(1)}, u32[]{:S(2)}, u32[]{:S(2)}) collective-permute-start(bf16[128,1024]{1,0:T(8,128)(2,1)S(1)} %get-tuple-element.27), channel_id=1, source_target_pairs={{0,8},{1,12},{2,0},{3,4},{4,1},{5,5},{6,16},{7,20},{8,17},{9,21},{... | collective-permute-start | bytes 786440 | tf_op jit(solution)/shard_map/ppermute | solution.py:274
  27.0 8.3 %collective-permute-done.refs_0_ = bf16[128,1024]{1,0:T(8,128)(2,1)S(1)} collective-permute-done((bf16[128,1024]{1,0:T(8,128)(2,1)S(1)}, bf16[128,1024]{1,0:T(8,128)(2,1)S(1)}, u32[]{:S(2)}, u32[]{:S(2)}) %collective-permute-start) | collective-permute-done | bytes 262176 | tf_op jit(solution)/shard_map/ppermute | solution.py:274
  35.3 8.5 %collective-permute-done.2.refs_2_ = bf16[128,1024]{1,0:T(8,128)(2,1)S(1)} collective-permute-done((bf16[128,1024]{1,0:T(8,128)(2,1)S(1)}, bf16[128,1024]{1,0:T(8,128)(2,1)S(1)}, u32[]{:S(2)}, u32[]{:S(2)}) %collective-permute-start.2) | collective-permute-done | bytes 262176 | tf_op jit(solution)/shard_map/ppermute | solution.py:274
  43.8 13.0 %collective-permute-done.3.refs_3_ = bf16[128,1024]{1,0:T(8,128)(2,1)S(1)} collective-permute-done((bf16[128,1024]{1,0:T(8,128)(2,1)S(1)}, bf16[128,1024]{1,0:T(8,128)(2,1)S(1)}, u32[]{:S(2)}, u32[]{:S(2)}) %collective-permute-start.3) | collective-permute-done | bytes 262176 | tf_op jit(solution)/shard_map/ppermute | solution.py:274
  67.0 9.5 %collective-permute-done.4 = bf16[128,2048]{1,0:T(8,128)(2,1)S(1)} collective-permute-done((bf16[128,2048]{1,0:T(8,128)(2,1)}, bf16[128,2048]{1,0:T(8,128)(2,1)S(1)}, u32[]{:S(2)}, u32[]{:S(2)}) %collective-permute-start.4) | collective-permute-done | bytes 524320 | tf_op jit(solution)/shard_map/ppermute | solution.py:290
  76.5 6.9 %collective-permute-done.5 = bf16[128,2048]{1,0:T(8,128)(2,1)S(1)} collective-permute-done((bf16[128,2048]{1,0:T(8,128)(2,1)}, bf16[128,2048]{1,0:T(8,128)(2,1)S(1)}, u32[]{:S(2)}, u32[]{:S(2)}) %collective-permute-start.5) | collective-permute-done | bytes 524320 | tf_op jit(solution)/shard_map/ppermute | solution.py:290
  86.0 7.4 %collective-permute-start.6 = (bf16[128,2048]{1,0:T(8,128)(2,1)S(1)}, bf16[128,2048]{1,0:T(8,128)(2,1)S(1)}, u32[]{:S(2)}, u32[]{:S(2)}) collective-permute-start(bf16[128,2048]{1,0:T(8,128)(2,1)S(1)} %copy-done.10), channel_id=1, source_target_pairs={{0,8},{8,16},{16,0},{1,9},{9,17},{17,1},{2,10},{10,18},{18,2},{3,1... | collective-permute-start | bytes 1572872 | tf_op jit(solution)/shard_map/ppermute | solution.py:290
  95.3 20.8 %collective-permute-done.6 = bf16[128,2048]{1,0:T(8,128)(2,1)S(1)} collective-permute-done((bf16[128,2048]{1,0:T(8,128)(2,1)S(1)}, bf16[128,2048]{1,0:T(8,128)(2,1)S(1)}, u32[]{:S(2)}, u32[]{:S(2)}) %collective-permute-start.6) | collective-permute-done | bytes 524320 | tf_op jit(solution)/shard_map/ppermute | solution.py:290
  135.2 5.2 %collective-permute-done.16.refs_1_ = bf16[384,512]{1,0:T(8,128)(2,1)S(1)} collective-permute-done((bf16[384,512]{1,0:T(8,128)(2,1)}, bf16[384,512]{1,0:T(8,128)(2,1)S(1)}, u32[]{:S(2)}, u32[]{:S(2)}) %collective-permute-start.16) | collective-permute-done | bytes 393248 | tf_op jit(solution)/shard_map/ppermute | solution.py:298
  140.4 7.9 %collective-permute-done.17.refs_2_ = bf16[384,512]{1,0:T(8,128)(2,1)S(1)} collective-permute-done((bf16[384,512]{1,0:T(8,128)(2,1)}, bf16[384,512]{1,0:T(8,128)(2,1)S(1)}, u32[]{:S(2)}, u32[]{:S(2)}) %collective-permute-start.17) | collective-permute-done | bytes 393248 | tf_op jit(solution)/shard_map/ppermute | solution.py:298
  155.1 11.0 %all-to-all-start.1 = ((bf16[32,48,128]{2,1,0:T(8,128)(2,1)}), bf16[32,48,128]{2,1,0:T(8,128)(2,1)S(1)}, u32[]{:S(2)}, u32[]{:S(2)}) async-start(bf16[32,48,128]{2,1,0:T(8,128)(2,1)} %bitcast.12), calls=%async_computation.1 | async-start | bytes 786432 | tf_op jit(solution)/shard_map/all_to_all | solution.py:302
  183.6 9.1 %collective-permute-done.20.refs_2_ = bf16[384,512]{1,0:T(8,128)(2,1)S(1)} collective-permute-done((bf16[384,512]{1,0:T(8,128)(2,1)}, bf16[384,512]{1,0:T(8,128)(2,1)S(1)}, u32[]{:S(2)}, u32[]{:S(2)}) %collective-permute-start.20) | collective-permute-done | bytes 393248 | tf_op jit(solution)/shard_map/ppermute | solution.py:298
  198.3 14.6 %all-to-all-start.2 = ((bf16[32,48,128]{2,1,0:T(8,128)(2,1)}), bf16[32,48,128]{2,1,0:T(8,128)(2,1)S(1)}, u32[]{:S(2)}, u32[]{:S(2)}) async-start(bf16[32,48,128]{2,1,0:T(8,128)(2,1)} %bitcast.11), calls=%async_computation.2 | async-start | bytes 786432 | tf_op jit(solution)/shard_map/all_to_all | solution.py:302
  213.6 6.4 %collective-permute-start.10 = (bf16[48,256]{1,0:T(8,128)(2,1)S(1)}, bf16[48,256]{1,0:T(8,128)(2,1)S(1)}, u32[]{:S(2)}, u32[]{:S(2)}) collective-permute-start(bf16[48,256]{1,0:T(8,128)(2,1)S(1)} %dynamic_slice.7.refs_0_), channel_id=1, source_target_pairs={{0,1},{1,2},{2,3},{3,0},{4,5},{5,6},{6,7},{7,4},{8,9},{9,10},{10,1... | collective-permute-start | bytes 73736 | tf_op jit(solution)/shard_map/ppermute | solution.py:279
  220.0 5.8 %collective-permute-start.11 = (bf16[48,256]{1,0:T(8,128)(2,1)S(1)}, bf16[48,256]{1,0:T(8,128)(2,1)S(1)}, u32[]{:S(2)}, u32[]{:S(2)}) collective-permute-start(bf16[48,256]{1,0:T(8,128)(2,1)S(1)} %dynamic_slice.7.refs_0_), channel_id=1, source_target_pairs={{0,2},{1,3},{2,0},{3,1},{4,6},{5,7},{6,4},{7,5},{8,10},{9,11},{10,... | collective-permute-start | bytes 73736 | tf_op jit(solution)/shard_map/ppermute | solution.py:279
  225.8 5.8 %collective-permute-start.12 = (bf16[48,256]{1,0:T(8,128)(2,1)S(1)}, bf16[48,256]{1,0:T(8,128)(2,1)S(1)}, u32[]{:S(2)}, u32[]{:S(2)}) collective-permute-start(bf16[48,256]{1,0:T(8,128)(2,1)S(1)} %dynamic_slice.7.refs_0_), channel_id=1, source_target_pairs={{0,3},{1,0},{2,1},{3,2},{4,7},{5,4},{6,5},{7,6},{8,11},{9,8},{10,9... | collective-permute-start | bytes 73736 | tf_op jit(solution)/shard_map/ppermute | solution.py:279
  237.2 7.2 %all-to-all-start = ((bf16[8,4,48,256]{3,2,1,0:T(8,128)(2,1)}), bf16[8,4,48,256]{3,2,1,0:T(8,128)(2,1)S(1)}, u32[]{:S(2)}, u32[]{:S(2)}) async-start(bf16[8,4,48,256]{3,2,1,0:T(8,128)(2,1)} %spread_cols.1), calls=%async_computation | async-start | bytes 1572864 | tf_op jit(solution)/shard_map/all_to_all | solution.py:281
  246.4 19.1 %all-to-all-done.src = bf16[8,4,48,256]{3,2,1,0:T(8,128)(2,1)S(1)} async-done(((bf16[8,4,48,256]{3,2,1,0:T(8,128)(2,1)}), bf16[8,4,48,256]{3,2,1,0:T(8,128)(2,1)S(1)}, u32[]{:S(2)}, u32[]{:S(2)}) %all-to-all-start) | async-done | bytes 786464 | tf_op jit(solution)/shard_map/all_to_all | solution.py:281
  285.4 6.1 %all-to-all-start.4 = ((bf16[4,2,384,128]{3,2,1,0:T(8,128)(2,1)}), bf16[4,2,384,128]{3,2,1,0:T(8,128)(2,1)S(1)}, u32[]{:S(2)}, u32[]{:S(2)}) async-start(bf16[4,2,384,128]{3,2,1,0:T(8,128)(2,1)} %spread_rows.1), calls=%async_computation.4 | async-start | bytes 1572864 | tf_op jit(solution)/shard_map/all_to_all | solution.py:306
  291.5 5.6 %collective-permute-done.13.refs_5_ = bf16[384,1024]{1,0:T(8,128)(2,1)S(1)} collective-permute-done((bf16[384,1024]{1,0:T(8,128)(2,1)}, bf16[384,1024]{1,0:T(8,128)(2,1)S(1)}, u32[]{:S(2)}, u32[]{:S(2)}) %collective-permute-start.13) | collective-permute-done | bytes 786464 | tf_op jit(solution)/shard_map/ppermute | solution.py:283
  297.1 17.3 %collective-permute-done.14.refs_6_ = bf16[384,1024]{1,0:T(8,128)(2,1)S(1)} collective-permute-done((bf16[384,1024]{1,0:T(8,128)(2,1)}, bf16[384,1024]{1,0:T(8,128)(2,1)S(1)}, u32[]{:S(2)}, u32[]{:S(2)}) %collective-permute-start.14) | collective-permute-done | bytes 786464 | tf_op jit(solution)/shard_map/ppermute | solution.py:283
  317.9 9.6 %heads_grad.1 = bf16[768,384]{1,0:T(8,128)(2,1)} custom-call(s32[1]{0:T(128)} %bitcast.at_ref, s32[6]{0:T(128)} %stack.34.rows_ref, bf16[384,2048]{1,0:T(8,128)(2,1)} %copy-done, bf16[384,2048]{1,0:T(8,128)(2,1)} %copy-done.1, bf16[384,2048]{1,0:T(8,128)(2,1)} %collective-permute-done.8.refs_2_.d, bf16[384,2048]{1,0:T(8,128)(2,1)} %collective-permute-done.9.refs_3_.d, ...), custom_call_target="tpu_custom_call" | custom-call | tf_op jit(solution)/shard_map/heads_grad/pallas_call | solution.py:168
  (102 shorter events, 104.0 us)
Async XLA Ops:
  2.8 32.5 %collective-permute-start = (bf16[128,1024]{1,0:T(8,128)(2,1)S(1)}, bf16[128,1024]{1,0:T(8,128)(2,1)S(1)}, u32[]{:S(2)}, u32[]{:S(2)}) collective-permute-start(bf16[128,1024]{1,0:T(8,128)(2,1)S(1)} %get-tuple-element.29), channel_id=1, source_target_pairs={{0,0},{1,4},{2,8},{3,12},{4,16},{5,20},{6,1},{7,5},{8,9},{9,13},{1... | collective-permute-start | bytes 786440 | tf_op jit(solution)/shard_map/ppermute | solution.py:274
  11.8 23.5 %collective-permute-start.1 = (bf16[128,1024]{1,0:T(8,128)(2,1)S(1)}, bf16[128,1024]{1,0:T(8,128)(2,1)S(1)}, u32[]{:S(2)}, u32[]{:S(2)}) collective-permute-start(bf16[128,1024]{1,0:T(8,128)(2,1)S(1)} %get-tuple-element.28), channel_id=1, source_target_pairs={{0,4},{1,8},{2,12},{3,0},{4,20},{5,1},{6,5},{7,16},{8,13},{9,17},{... | collective-permute-start | bytes 786440 | tf_op jit(solution)/shard_map/ppermute | solution.py:274
  17.1 26.7 %collective-permute-start.2 = (bf16[128,1024]{1,0:T(8,128)(2,1)S(1)}, bf16[128,1024]{1,0:T(8,128)(2,1)S(1)}, u32[]{:S(2)}, u32[]{:S(2)}) collective-permute-start(bf16[128,1024]{1,0:T(8,128)(2,1)S(1)} %get-tuple-element.27), channel_id=1, source_target_pairs={{0,8},{1,12},{2,0},{3,4},{4,1},{5,5},{6,16},{7,20},{8,17},{9,21},{... | collective-permute-start | bytes 786440 | tf_op jit(solution)/shard_map/ppermute | solution.py:274
  23.2 33.6 %collective-permute-start.3 = (bf16[128,1024]{1,0:T(8,128)(2,1)S(1)}, bf16[128,1024]{1,0:T(8,128)(2,1)S(1)}, u32[]{:S(2)}, u32[]{:S(2)}) collective-permute-start(bf16[128,1024]{1,0:T(8,128)(2,1)S(1)} %get-tuple-element.26), channel_id=1, source_target_pairs={{0,12},{1,0},{2,4},{3,8},{4,5},{5,16},{6,20},{7,1},{8,21},{9,9},{1... | collective-permute-start | bytes 786440 | tf_op jit(solution)/shard_map/ppermute | solution.py:274
  59.9 16.6 %collective-permute-start.4 = (bf16[128,2048]{1,0:T(8,128)(2,1)}, bf16[128,2048]{1,0:T(8,128)(2,1)S(1)}, u32[]{:S(2)}, u32[]{:S(2)}) collective-permute-start(bf16[128,2048]{1,0:T(8,128)(2,1)} %get-tuple-element.14), channel_id=1, source_target_pairs={{0,8},{8,16},{16,0},{1,9},{9,17},{17,1},{2,10},{10,18},{18,2},{3,1... | collective-permute-start | bytes 1572872 | tf_op jit(solution)/shard_map/ppermute | solution.py:290
  62.0 21.5 %collective-permute-start.5 = (bf16[128,2048]{1,0:T(8,128)(2,1)}, bf16[128,2048]{1,0:T(8,128)(2,1)S(1)}, u32[]{:S(2)}, u32[]{:S(2)}) collective-permute-start(bf16[128,2048]{1,0:T(8,128)(2,1)} %get-tuple-element.14), channel_id=1, source_target_pairs={{0,16},{8,0},{16,8},{1,17},{9,1},{17,9},{2,18},{10,2},{18,10},{3,1... | collective-permute-start | bytes 1572872 | tf_op jit(solution)/shard_map/ppermute | solution.py:290
  83.5 38.1 %collective-permute-start.8 = (bf16[384,2048]{1,0:T(8,128)(2,1)S(1)}, bf16[384,2048]{1,0:T(8,128)(2,1)}, u32[]{:S(2)}, u32[]{:S(2)}) collective-permute-start(bf16[384,2048]{1,0:T(8,128)(2,1)S(1)} %constant_dynamic-update-slice_fusion.refs_0_.c), channel_id=1, source_target_pairs={{0,4},{4,0},{1,5},{5,1},{2,6},{6,2},{3,7},{7,3},{8,12},{12,8},{9,1... | collective-permute-start | bytes 4718600 | tf_op jit(solution)/shard_map/ppermute | solution.py:294
  86.0 30.1 %collective-permute-start.6 = (bf16[128,2048]{1,0:T(8,128)(2,1)S(1)}, bf16[128,2048]{1,0:T(8,128)(2,1)S(1)}, u32[]{:S(2)}, u32[]{:S(2)}) collective-permute-start(bf16[128,2048]{1,0:T(8,128)(2,1)S(1)} %copy-done.10), channel_id=1, source_target_pairs={{0,8},{8,16},{16,0},{1,9},{9,17},{17,1},{2,10},{10,18},{18,2},{3,1... | collective-permute-start | bytes 1572872 | tf_op jit(solution)/shard_map/ppermute | solution.py:290
  93.4 23.6 %collective-permute-start.7 = (bf16[128,2048]{1,0:T(8,128)(2,1)S(1)}, bf16[128,2048]{1,0:T(8,128)(2,1)S(1)}, u32[]{:S(2)}, u32[]{:S(2)}) collective-permute-start(bf16[128,2048]{1,0:T(8,128)(2,1)S(1)} %copy-done.10), channel_id=1, source_target_pairs={{0,16},{8,0},{16,8},{1,17},{9,1},{17,9},{2,18},{10,2},{18,10},{3,1... | collective-permute-start | bytes 1572872 | tf_op jit(solution)/shard_map/ppermute | solution.py:290
  117.0 49.2 %collective-permute-start.9 = (bf16[384,2048]{1,0:T(8,128)(2,1)S(1)}, bf16[384,2048]{1,0:T(8,128)(2,1)}, u32[]{:S(2)}, u32[]{:S(2)}) collective-permute-start(bf16[384,2048]{1,0:T(8,128)(2,1)S(1)} %constant_dynamic-update-slice_fusion.3.refs_1_.c), channel_id=1, source_target_pairs={{0,4},{4,0},{1,5},{5,1},{2,6},{6,2},{3,7},{7,3},{8,12},{12,8},{9,1... | collective-permute-start | bytes 4718600 | tf_op jit(solution)/shard_map/ppermute | solution.py:294
  129.4 18.9 %collective-permute-start.17 = (bf16[384,512]{1,0:T(8,128)(2,1)}, bf16[384,512]{1,0:T(8,128)(2,1)S(1)}, u32[]{:S(2)}, u32[]{:S(2)}) collective-permute-start(bf16[384,512]{1,0:T(8,128)(2,1)} %get-tuple-element.20), channel_id=1, source_target_pairs={{0,48},{24,72},{48,0},{72,24},{1,49},{25,73},{49,1},{73,25},{2,50}... | collective-permute-start | bytes 1179656 | tf_op jit(solution)/shard_map/ppermute | solution.py:298
  132.1 20.0 %collective-permute-start.18 = (bf16[384,512]{1,0:T(8,128)(2,1)}, bf16[384,512]{1,0:T(8,128)(2,1)S(1)}, u32[]{:S(2)}, u32[]{:S(2)}) collective-permute-start(bf16[384,512]{1,0:T(8,128)(2,1)} %get-tuple-element.21), channel_id=1, source_target_pairs={{0,72},{24,0},{48,24},{72,48},{1,73},{25,1},{49,25},{73,49},{2,74}... | collective-permute-start | bytes 1179656 | tf_op jit(solution)/shard_map/ppermute | solution.py:298
  155.1 43.2 %all-to-all-start.1 = ((bf16[32,48,128]{2,1,0:T(8,128)(2,1)}), bf16[32,48,128]{2,1,0:T(8,128)(2,1)S(1)}, u32[]{:S(2)}, u32[]{:S(2)}) async-start(bf16[32,48,128]{2,1,0:T(8,128)(2,1)} %bitcast.12), calls=%async_computation.1 | async-start | bytes 786432 | tf_op jit(solution)/shard_map/all_to_all | solution.py:302
  173.8 18.9 %collective-permute-start.20 = (bf16[384,512]{1,0:T(8,128)(2,1)}, bf16[384,512]{1,0:T(8,128)(2,1)S(1)}, u32[]{:S(2)}, u32[]{:S(2)}) collective-permute-start(bf16[384,512]{1,0:T(8,128)(2,1)} %get-tuple-element.24), channel_id=1, source_target_pairs={{0,48},{24,72},{48,0},{72,24},{1,49},{25,73},{49,1},{73,25},{2,50}... | collective-permute-start | bytes 1179656 | tf_op jit(solution)/shard_map/ppermute | solution.py:298
  177.5 17.7 %collective-permute-start.21 = (bf16[384,512]{1,0:T(8,128)(2,1)}, bf16[384,512]{1,0:T(8,128)(2,1)S(1)}, u32[]{:S(2)}, u32[]{:S(2)}) collective-permute-start(bf16[384,512]{1,0:T(8,128)(2,1)} %get-tuple-element.25), channel_id=1, source_target_pairs={{0,72},{24,0},{48,24},{72,48},{1,73},{25,1},{49,25},{73,49},{2,74}... | collective-permute-start | bytes 1179656 | tf_op jit(solution)/shard_map/ppermute | solution.py:298
  198.3 38.9 %all-to-all-start.2 = ((bf16[32,48,128]{2,1,0:T(8,128)(2,1)}), bf16[32,48,128]{2,1,0:T(8,128)(2,1)S(1)}, u32[]{:S(2)}, u32[]{:S(2)}) async-start(bf16[32,48,128]{2,1,0:T(8,128)(2,1)} %bitcast.11), calls=%async_computation.2 | async-start | bytes 786432 | tf_op jit(solution)/shard_map/all_to_all | solution.py:302
  213.6 18.1 %collective-permute-start.10 = (bf16[48,256]{1,0:T(8,128)(2,1)S(1)}, bf16[48,256]{1,0:T(8,128)(2,1)S(1)}, u32[]{:S(2)}, u32[]{:S(2)}) collective-permute-start(bf16[48,256]{1,0:T(8,128)(2,1)S(1)} %dynamic_slice.7.refs_0_), channel_id=1, source_target_pairs={{0,1},{1,2},{2,3},{3,0},{4,5},{5,6},{6,7},{7,4},{8,9},{9,10},{10,1... | collective-permute-start | bytes 73736 | tf_op jit(solution)/shard_map/ppermute | solution.py:279
  220.0 14.7 %collective-permute-start.11 = (bf16[48,256]{1,0:T(8,128)(2,1)S(1)}, bf16[48,256]{1,0:T(8,128)(2,1)S(1)}, u32[]{:S(2)}, u32[]{:S(2)}) collective-permute-start(bf16[48,256]{1,0:T(8,128)(2,1)S(1)} %dynamic_slice.7.refs_0_), channel_id=1, source_target_pairs={{0,2},{1,3},{2,0},{3,1},{4,6},{5,7},{6,4},{7,5},{8,10},{9,11},{10,... | collective-permute-start | bytes 73736 | tf_op jit(solution)/shard_map/ppermute | solution.py:279
  237.2 28.2 %all-to-all-start = ((bf16[8,4,48,256]{3,2,1,0:T(8,128)(2,1)}), bf16[8,4,48,256]{3,2,1,0:T(8,128)(2,1)S(1)}, u32[]{:S(2)}, u32[]{:S(2)}) async-start(bf16[8,4,48,256]{3,2,1,0:T(8,128)(2,1)} %spread_cols.1), calls=%async_computation | async-start | bytes 1572864 | tf_op jit(solution)/shard_map/all_to_all | solution.py:281
  265.5 17.3 %all-to-all-start.3 = ((bf16[8,2,48,128]{3,2,1,0:T(8,128)(2,1)}), bf16[8,2,48,128]{3,2,1,0:T(8,128)(2,1)S(1)}, u32[]{:S(2)}, u32[]{:S(2)}) async-start(bf16[8,2,48,128]{3,2,1,0:T(8,128)(2,1)} %spread_sum.1), calls=%async_computation.3 | async-start | bytes 393216 | tf_op jit(solution)/shard_map/all_to_all | solution.py:304
  272.4 24.7 %collective-permute-start.13 = (bf16[384,1024]{1,0:T(8,128)(2,1)}, bf16[384,1024]{1,0:T(8,128)(2,1)S(1)}, u32[]{:S(2)}, u32[]{:S(2)}) collective-permute-start(bf16[384,1024]{1,0:T(8,128)(2,1)} %weight_rows.1.refs_4_), channel_id=1, source_target_pairs={{0,24},{24,48},{48,72},{72,0},{1,25},{25,49},{49,73},{73,1},{2,26}... | collective-permute-start | bytes 2359304 | tf_op jit(solution)/shard_map/ppermute | solution.py:283
  277.1 37.3 %collective-permute-start.14 = (bf16[384,1024]{1,0:T(8,128)(2,1)}, bf16[384,1024]{1,0:T(8,128)(2,1)S(1)}, u32[]{:S(2)}, u32[]{:S(2)}) collective-permute-start(bf16[384,1024]{1,0:T(8,128)(2,1)} %weight_rows.1.refs_4_), channel_id=1, source_target_pairs={{0,48},{24,72},{48,0},{72,24},{1,49},{25,73},{49,1},{73,25},{2,50}... | collective-permute-start | bytes 2359304 | tf_op jit(solution)/shard_map/ppermute | solution.py:283
  280.8 36.1 %collective-permute-start.15 = (bf16[384,1024]{1,0:T(8,128)(2,1)}, bf16[384,1024]{1,0:T(8,128)(2,1)S(1)}, u32[]{:S(2)}, u32[]{:S(2)}) collective-permute-start(bf16[384,1024]{1,0:T(8,128)(2,1)} %weight_rows.1.refs_4_), channel_id=1, source_target_pairs={{0,72},{24,0},{48,24},{72,48},{1,73},{25,1},{49,25},{73,49},{2,74}... | collective-permute-start | bytes 2359304 | tf_op jit(solution)/shard_map/ppermute | solution.py:283
  285.4 42.2 %all-to-all-start.4 = ((bf16[4,2,384,128]{3,2,1,0:T(8,128)(2,1)}), bf16[4,2,384,128]{3,2,1,0:T(8,128)(2,1)S(1)}, u32[]{:S(2)}, u32[]{:S(2)}) async-start(bf16[4,2,384,128]{3,2,1,0:T(8,128)(2,1)} %spread_rows.1), calls=%async_computation.4 | async-start | bytes 1572864 | tf_op jit(solution)/shard_map/all_to_all | solution.py:306
  (28 other events, 294.0 us)

commit v2 on v1

--- a/solution.py
+++ b/solution.py
@@ -198,23 +198,39 @@
     )(*parts)
 
 
-def spread_sum(parts):
-    shape = (Y, CHUNKS) + parts[0].shape[1:]
+def sum_rows(parts):
+    _, _, rows, _ = parts[0].shape
 
     def kernel(*refs):
         out = refs[-1]
         for h in range(CHUNKS):
-            total = jnp.sum(refs[h][...].astype(jnp.float32), axis=0).astype(out.dtype)
-            for y in range(Y):
-                out[y, h] = total
-
-    return pl.pallas_call(
-        kernel,
-        out_shape=jax.ShapeDtypeStruct(shape, parts[0].dtype),
+            for col in range(ZH):
+                out[col, h] = jnp.sum(refs[h][:, col].astype(jnp.float32), axis=0).astype(out.dtype)
+
+    return pl.pallas_call(
+        kernel,
+        out_shape=jax.ShapeDtypeStruct((ZH, CHUNKS, rows, LANE), parts[0].dtype),
         in_specs=[VMEM] * CHUNKS,
         out_specs=VMEM,
+        name="sum_rows",
+    )(*parts)
+
+
+def spread_sum(parts):
+    shape = (Y,) + parts.shape[1:]
+
+    def kernel(src, out):
+        total = jnp.sum(src[...].astype(jnp.float32), axis=0).astype(out.dtype)
+        for y in range(Y):
+            out[y] = total
+
+    return pl.pallas_call(
+        kernel,
+        out_shape=jax.ShapeDtypeStruct(shape, parts.dtype),
+        in_specs=[VMEM],
+        out_specs=VMEM,
         name="spread_sum",
-    )(*parts)
+    )(parts)
 
 
 def spread_rows(parts):
@@ -268,11 +284,8 @@
 
     rows = [[order(zl, c), order(zl + 2, c), order(zl + 1, c)] for c in (core, 1 - core)]
 
-    cot2 = jnp.concatenate([cot, cot], axis=0)
-    cot_sends = lax.dynamic_slice(cot2, (zh * blk, 0), (tok, feat))
-    got = [
-        lax.ppermute(cot_sends[k * blk:(k + 1) * blk], ("zl", "core", "zh"), spread_pairs(k)) for k in range(ZH)
-    ]
+    sends = [lax.dynamic_slice(cot, ((zh + k) % ZH * blk, 0), (blk, feat)) for k in range(ZH)]
+    got = [lax.ppermute(sends[k], ("zl", "core", "zh"), spread_pairs(k)) for k in range(ZH)]
 
     wr, wc = hid // Y, feat // X
     w_part = lax.dynamic_slice(weight, (yi * wr, xi * wc), (wr, wc))
@@ -299,8 +312,10 @@
     sums = []
     for h in range(CHUNKS):
         r = sum_split(parts[h])
-        sums.append(lax.all_to_all(r.reshape((Y * ZH,) + r.shape[2:]), ("y", "zh"), 0, 0))
-    r = spread_sum(sums)
+        sums.append(lax.all_to_all(r, "y", 0, 0))
+    r = sum_rows(sums)
+    r = lax.all_to_all(r, "zh", 0, 0)
+    r = spread_sum(r)
     r = lax.all_to_all(r, "y", 0, 0)
     r = spread_rows(r)
     r = lax.all_to_all(r, "x", 0, 0)

time: 332 us -> 327 us (0.985)
  the two profiles are of different devices: /device:TPU:76 before, /device:TPU:8 now
where the time goes in v2:
time: 327 us; the launch traced here: 325 us
  starting transfers between devices  135 us (41%)
  waiting for transfers between devices  121 us (37%)
  Pallas kernels  39.5 us (12%)
  blocking collectives  19.8 us (6%)
  local copies, waits for them, and re-layouts  9.43 us (3%)
    ppermute x4, waiting for transfers between devices, per_device(): lax.ppermute(mine[h], 'zl', ring(ZL, k))  33.3 us
    ppermute x6, waiting for transfers between devices, per_device(): lax.ppermute(part[k], 'x', ring(X, k))  26.9 us
    ppermute x4, starting transfers between devices, per_device(): lax.ppermute(sends[k], ('zl', 'core', 'zh'), spread_pairs(k))  26.9 us
    ppermute x3, waiting for transfers between devices, per_device(): w_x = [w_y] + [lax.ppermute(w_y, 'x', ring(X, k)) for k in range(1, X)]  25.5 us
    ppermute x4, starting transfers between devices, per_device(): lax.ppermute(mine[h], 'zl', ring(ZL, k))  23.2 us
    ppermute x6, starting transfers between devices, per_device(): lax.ppermute(part[k], 'x', ring(X, k))  22.7 us
    all_to_all x1, blocking collectives, per_device(): sums.append(lax.all_to_all(r, 'y', 0, 0))  19.8 us
    ppermute x3, starting transfers between devices, per_device(): w_far = [lax.ppermute(w_part, 'zh', ring(ZH, k)) for k in range(1, ZH)]  18.5 us
  transfers between devices with their start and end apart: 27, of which 16 were waited for; matrix products, arithmetic and copies ran while one was open for 1% of the time, Pallas kernels for 10%

profile of v2, /device:TPU:8, one launch (start us, length us, event | category | flops | bytes accessed | tf_op | source)
XLA Modules:
  0.0 325.5 jit_solution(4849879693030577087)
XLA Ops:
  2.6 7.4 %collective-permute-start.1 = (bf16[128,1024]{1,0:T(8,128)(2,1)S(1)}, bf16[128,1024]{1,0:T(8,128)(2,1)S(1)}, u32[]{:S(2)}, u32[]{:S(2)}) collective-permute-start(bf16[128,1024]{1,0:T(8,128)(2,1)S(1)} %get-tuple-element.27), channel_id=1, source_target_pairs={{0,4},{1,8},{2,12},{3,0},{4,20},{5,1},{6,5},{7,16},{8,13},{9,17},{... | collective-permute-start | bytes 786440 | tf_op jit(solution)/shard_map/ppermute | solution.py:288
  10.1 10.5 %collective-permute-start.2 = (bf16[128,1024]{1,0:T(8,128)(2,1)S(1)}, bf16[128,1024]{1,0:T(8,128)(2,1)S(1)}, u32[]{:S(2)}, u32[]{:S(2)}) collective-permute-start(bf16[128,1024]{1,0:T(8,128)(2,1)S(1)} %get-tuple-element.29), channel_id=1, source_target_pairs={{0,8},{1,12},{2,0},{3,4},{4,1},{5,5},{6,16},{7,20},{8,17},{9,21},{... | collective-permute-start | bytes 786440 | tf_op jit(solution)/shard_map/ppermute | solution.py:288
  20.6 8.2 %collective-permute-start.3 = (bf16[128,1024]{1,0:T(8,128)(2,1)S(1)}, bf16[128,1024]{1,0:T(8,128)(2,1)S(1)}, u32[]{:S(2)}, u32[]{:S(2)}) collective-permute-start(bf16[128,1024]{1,0:T(8,128)(2,1)S(1)} %get-tuple-element.26), channel_id=1, source_target_pairs={{0,12},{1,0},{2,4},{3,8},{4,5},{5,16},{6,20},{7,1},{8,21},{9,9},{1... | collective-permute-start | bytes 786440 | tf_op jit(solution)/shard_map/ppermute | solution.py:288
  28.9 16.8 %collective-permute-done.2.refs_2_ = bf16[128,1024]{1,0:T(8,128)(2,1)S(1)} collective-permute-done((bf16[128,1024]{1,0:T(8,128)(2,1)S(1)}, bf16[128,1024]{1,0:T(8,128)(2,1)S(1)}, u32[]{:S(2)}, u32[]{:S(2)}) %collective-permute-start.2) | collective-permute-done | bytes 262176 | tf_op jit(solution)/shard_map/ppermute | solution.py:288
  49.0 14.4 %collective-permute-start.4 = (bf16[128,2048]{1,0:T(8,128)(2,1)}, bf16[128,2048]{1,0:T(8,128)(2,1)S(1)}, u32[]{:S(2)}, u32[]{:S(2)}) collective-permute-start(bf16[128,2048]{1,0:T(8,128)(2,1)} %get-tuple-element.14), channel_id=1, source_target_pairs={{0,8},{8,16},{16,0},{1,9},{9,17},{17,1},{2,10},{10,18},{18,2},{3,1... | collective-permute-start | bytes 1572872 | tf_op jit(solution)/shard_map/ppermute | solution.py:303
  75.6 15.8 %collective-permute-done.5 = bf16[128,2048]{1,0:T(8,128)(2,1)S(1)} collective-permute-done((bf16[128,2048]{1,0:T(8,128)(2,1)}, bf16[128,2048]{1,0:T(8,128)(2,1)S(1)}, u32[]{:S(2)}, u32[]{:S(2)}) %collective-permute-start.5) | collective-permute-done | bytes 524320 | tf_op jit(solution)/shard_map/ppermute | solution.py:303
  98.1 11.2 %collective-permute-done.7 = bf16[128,2048]{1,0:T(8,128)(2,1)S(1)} collective-permute-done((bf16[128,2048]{1,0:T(8,128)(2,1)}, bf16[128,2048]{1,0:T(8,128)(2,1)S(1)}, u32[]{:S(2)}, u32[]{:S(2)}) %collective-permute-start.7) | collective-permute-done | bytes 524320 | tf_op jit(solution)/shard_map/ppermute | solution.py:303
  122.6 4.6 %collective-permute-start.17 = (bf16[384,512]{1,0:T(8,128)(2,1)}, bf16[384,512]{1,0:T(8,128)(2,1)S(1)}, u32[]{:S(2)}, u32[]{:S(2)}) collective-permute-start(bf16[384,512]{1,0:T(8,128)(2,1)} %get-tuple-element.20), channel_id=1, source_target_pairs={{0,48},{24,72},{48,0},{72,24},{1,49},{25,73},{49,1},{73,25},{2,50}... | collective-permute-start | bytes 1179656 | tf_op jit(solution)/shard_map/ppermute | solution.py:311
  133.5 9.4 %collective-permute-done.17.refs_2_ = bf16[384,512]{1,0:T(8,128)(2,1)S(1)} collective-permute-done((bf16[384,512]{1,0:T(8,128)(2,1)}, bf16[384,512]{1,0:T(8,128)(2,1)S(1)}, u32[]{:S(2)}, u32[]{:S(2)}) %collective-permute-start.17) | collective-permute-done | bytes 393248 | tf_op jit(solution)/shard_map/ppermute | solution.py:311
  147.6 7.5 %all-to-all-start.1 = ((bf16[8,4,48,128]{3,2,1,0:T(8,128)(2,1)}), bf16[8,4,48,128]{3,2,1,0:T(8,128)(2,1)S(1)}, u32[]{:S(2)}, u32[]{:S(2)}) async-start(bf16[8,4,48,128]{3,2,1,0:T(8,128)(2,1)} %sum_split.2), calls=%async_computation.1 | async-start | bytes 786432 | tf_op jit(solution)/shard_map/all_to_all | solution.py:315
  155.1 4.6 %weight_part.3 = (bf16[384,512]{1,0:T(8,128)(2,1)}, bf16[384,512]{1,0:T(8,128)(2,1)}, bf16[384,512]{1,0:T(8,128)(2,1)}, bf16[384,512]{1,0:T(8,128)(2,1)}) custom-call(s32[1]{0:T(128)} %bitcast.at_ref, bf16[384,384]{1,0:T(8,128)(2,1)} %get-tuple-element.16.a, bf16[384,384]{1,0:T(8,128)(2,1)} %get-tuple-element.17.b, bf16[384,2048]{1,0:T(8,128)(2,1)} %copy-done.1, ...), custom_call_target="tpu_custom_call" | custom-call | tf_op jit(solution)/shard_map/weight_part/pallas_call | solution.py:133
  173.8 9.0 %collective-permute-done.20.refs_2_ = bf16[384,512]{1,0:T(8,128)(2,1)S(1)} collective-permute-done((bf16[384,512]{1,0:T(8,128)(2,1)}, bf16[384,512]{1,0:T(8,128)(2,1)S(1)}, u32[]{:S(2)}, u32[]{:S(2)}) %collective-permute-start.20) | collective-permute-done | bytes 393248 | tf_op jit(solution)/shard_map/ppermute | solution.py:311
  187.2 19.8 %all_to_all.30.refs_1_ = bf16[8,4,48,128]{3,2,1,0:T(8,128)(2,1)} all-to-all(bf16[8,4,48,128]{3,2,1,0:T(8,128)(2,1)} %sum_split.3), channel_id=1, replica_groups=mesh['y'=8,'x'=4,'zl'=3,'core'=2,'zh'=4] {'y'}, dimensions={0} | all-to-all | bytes 786432 | tf_op jit(solution)/shard_map/all_to_all | solution.py:315
  208.8 5.0 %all-to-all-start.3 = ((bf16[4,2,48,128]{3,2,1,0:T(8,128)(2,1)}), bf16[4,2,48,128]{3,2,1,0:T(8,128)(2,1)S(1)}, u32[]{:S(2)}, u32[]{:S(2)}) async-start(bf16[4,2,48,128]{3,2,1,0:T(8,128)(2,1)} %sum_rows.1), calls=%async_computation.3 | async-start | bytes 196608 | tf_op jit(solution)/shard_map/all_to_all | solution.py:317
  214.6 5.7 %collective-permute-start.10 = (bf16[48,256]{1,0:T(8,128)(2,1)S(1)}, bf16[48,256]{1,0:T(8,128)(2,1)S(1)}, u32[]{:S(2)}, u32[]{:S(2)}) collective-permute-start(bf16[48,256]{1,0:T(8,128)(2,1)S(1)} %dynamic_slice.19.refs_0_), channel_id=1, source_target_pairs={{0,1},{1,2},{2,3},{3,0},{4,5},{5,6},{6,7},{7,4},{8,9},{9,10},{10,1... | collective-permute-start | bytes 73736 | tf_op jit(solution)/shard_map/ppermute | solution.py:292
  220.3 7.6 %collective-permute-start.11 = (bf16[48,256]{1,0:T(8,128)(2,1)S(1)}, bf16[48,256]{1,0:T(8,128)(2,1)S(1)}, u32[]{:S(2)}, u32[]{:S(2)}) collective-permute-start(bf16[48,256]{1,0:T(8,128)(2,1)S(1)} %dynamic_slice.19.refs_0_), channel_id=1, source_target_pairs={{0,2},{1,3},{2,0},{3,1},{4,6},{5,7},{6,4},{7,5},{8,10},{9,11},{10,... | collective-permute-start | bytes 73736 | tf_op jit(solution)/shard_map/ppermute | solution.py:292
  227.9 5.2 %collective-permute-start.12 = (bf16[48,256]{1,0:T(8,128)(2,1)S(1)}, bf16[48,256]{1,0:T(8,128)(2,1)S(1)}, u32[]{:S(2)}, u32[]{:S(2)}) collective-permute-start(bf16[48,256]{1,0:T(8,128)(2,1)S(1)} %dynamic_slice.19.refs_0_), channel_id=1, source_target_pairs={{0,3},{1,0},{2,1},{3,2},{4,7},{5,4},{6,5},{7,6},{8,11},{9,8},{10,9... | collective-permute-start | bytes 73736 | tf_op jit(solution)/shard_map/ppermute | solution.py:292
  237.9 4.9 %all-to-all-start = ((bf16[8,4,48,256]{3,2,1,0:T(8,128)(2,1)}), bf16[8,4,48,256]{3,2,1,0:T(8,128)(2,1)S(1)}, u32[]{:S(2)}, u32[]{:S(2)}) async-start(bf16[8,4,48,256]{3,2,1,0:T(8,128)(2,1)} %spread_cols.1), calls=%async_computation | async-start | bytes 1572864 | tf_op jit(solution)/shard_map/all_to_all | solution.py:294
  244.4 16.1 %all-to-all-done.src = bf16[8,4,48,256]{3,2,1,0:T(8,128)(2,1)S(1)} async-done(((bf16[8,4,48,256]{3,2,1,0:T(8,128)(2,1)}), bf16[8,4,48,256]{3,2,1,0:T(8,128)(2,1)S(1)}, u32[]{:S(2)}, u32[]{:S(2)}) %all-to-all-start) | async-done | bytes 786464 | tf_op jit(solution)/shard_map/all_to_all | solution.py:294
  260.4 4.8 %all-to-all-start.4 = ((bf16[8,2,48,128]{3,2,1,0:T(8,128)(2,1)}), bf16[8,2,48,128]{3,2,1,0:T(8,128)(2,1)S(1)}, u32[]{:S(2)}, u32[]{:S(2)}) async-start(bf16[8,2,48,128]{3,2,1,0:T(8,128)(2,1)} %spread_sum.1), calls=%async_computation.4 | async-start | bytes 393216 | tf_op jit(solution)/shard_map/all_to_all | solution.py:319
  267.4 6.1 %collective-permute-start.13 = (bf16[384,1024]{1,0:T(8,128)(2,1)}, bf16[384,1024]{1,0:T(8,128)(2,1)S(1)}, u32[]{:S(2)}, u32[]{:S(2)}) collective-permute-start(bf16[384,1024]{1,0:T(8,128)(2,1)} %weight_rows.1.refs_4_), channel_id=1, source_target_pairs={{0,24},{24,48},{48,72},{72,0},{1,25},{25,49},{49,73},{73,1},{2,26}... | collective-permute-start | bytes 2359304 | tf_op jit(solution)/shard_map/ppermute | solution.py:296
  286.1 17.2 %collective-permute-done.13.refs_5_ = bf16[384,1024]{1,0:T(8,128)(2,1)S(1)} collective-permute-done((bf16[384,1024]{1,0:T(8,128)(2,1)}, bf16[384,1024]{1,0:T(8,128)(2,1)S(1)}, u32[]{:S(2)}, u32[]{:S(2)}) %collective-permute-start.13) | collective-permute-done | bytes 786464 | tf_op jit(solution)/shard_map/ppermute | solution.py:296
  303.4 7.0 %collective-permute-done.14.refs_6_ = bf16[384,1024]{1,0:T(8,128)(2,1)S(1)} collective-permute-done((bf16[384,1024]{1,0:T(8,128)(2,1)}, bf16[384,1024]{1,0:T(8,128)(2,1)S(1)}, u32[]{:S(2)}, u32[]{:S(2)}) %collective-permute-start.14) | collective-permute-done | bytes 786464 | tf_op jit(solution)/shard_map/ppermute | solution.py:296
  312.7 9.6 %heads_grad.1 = bf16[768,384]{1,0:T(8,128)(2,1)} custom-call(s32[1]{0:T(128)} %bitcast.at_ref, s32[6]{0:T(128)} %stack.34.rows_ref, bf16[384,2048]{1,0:T(8,128)(2,1)} %copy-done, bf16[384,2048]{1,0:T(8,128)(2,1)} %copy-done.1, bf16[384,2048]{1,0:T(8,128)(2,1)} %collective-permute-done.8.refs_2_.d, bf16[384,2048]{1,0:T(8,128)(2,1)} %collective-permute-done.9.refs_3_.d, ...), custom_call_target="tpu_custom_call" | custom-call | tf_op jit(solution)/shard_map/heads_grad/pallas_call | solution.py:168
  (103 shorter events, 95.7 us)
Async XLA Ops:
  2.0 26.9 %collective-permute-start = (bf16[128,1024]{1,0:T(8,128)(2,1)S(1)}, bf16[128,1024]{1,0:T(8,128)(2,1)S(1)}, u32[]{:S(2)}, u32[]{:S(2)}) collective-permute-start(bf16[128,1024]{1,0:T(8,128)(2,1)S(1)} %get-tuple-element.28), channel_id=1, source_target_pairs={{0,0},{1,4},{2,8},{3,12},{4,16},{5,20},{6,1},{7,5},{8,9},{9,13},{1... | collective-permute-start | bytes 786440 | tf_op jit(solution)/shard_map/ppermute | solution.py:288
  2.6 26.3 %collective-permute-start.1 = (bf16[128,1024]{1,0:T(8,128)(2,1)S(1)}, bf16[128,1024]{1,0:T(8,128)(2,1)S(1)}, u32[]{:S(2)}, u32[]{:S(2)}) collective-permute-start(bf16[128,1024]{1,0:T(8,128)(2,1)S(1)} %get-tuple-element.27), channel_id=1, source_target_pairs={{0,4},{1,8},{2,12},{3,0},{4,20},{5,1},{6,5},{7,16},{8,13},{9,17},{... | collective-permute-start | bytes 786440 | tf_op jit(solution)/shard_map/ppermute | solution.py:288
  10.1 35.7 %collective-permute-start.2 = (bf16[128,1024]{1,0:T(8,128)(2,1)S(1)}, bf16[128,1024]{1,0:T(8,128)(2,1)S(1)}, u32[]{:S(2)}, u32[]{:S(2)}) collective-permute-start(bf16[128,1024]{1,0:T(8,128)(2,1)S(1)} %get-tuple-element.29), channel_id=1, source_target_pairs={{0,8},{1,12},{2,0},{3,4},{4,1},{5,5},{6,16},{7,20},{8,17},{9,21},{... | collective-permute-start | bytes 786440 | tf_op jit(solution)/shard_map/ppermute | solution.py:288
  20.6 25.1 %collective-permute-start.3 = (bf16[128,1024]{1,0:T(8,128)(2,1)S(1)}, bf16[128,1024]{1,0:T(8,128)(2,1)S(1)}, u32[]{:S(2)}, u32[]{:S(2)}) collective-permute-start(bf16[128,1024]{1,0:T(8,128)(2,1)S(1)} %get-tuple-element.26), channel_id=1, source_target_pairs={{0,12},{1,0},{2,4},{3,8},{4,5},{5,16},{6,20},{7,1},{8,21},{9,9},{1... | collective-permute-start | bytes 786440 | tf_op jit(solution)/shard_map/ppermute | solution.py:288
  49.0 26.5 %collective-permute-start.4 = (bf16[128,2048]{1,0:T(8,128)(2,1)}, bf16[128,2048]{1,0:T(8,128)(2,1)S(1)}, u32[]{:S(2)}, u32[]{:S(2)}) collective-permute-start(bf16[128,2048]{1,0:T(8,128)(2,1)} %get-tuple-element.14), channel_id=1, source_target_pairs={{0,8},{8,16},{16,0},{1,9},{9,17},{17,1},{2,10},{10,18},{18,2},{3,1... | collective-permute-start | bytes 1572872 | tf_op jit(solution)/shard_map/ppermute | solution.py:303
  63.4 27.9 %collective-permute-start.5 = (bf16[128,2048]{1,0:T(8,128)(2,1)}, bf16[128,2048]{1,0:T(8,128)(2,1)S(1)}, u32[]{:S(2)}, u32[]{:S(2)}) collective-permute-start(bf16[128,2048]{1,0:T(8,128)(2,1)} %get-tuple-element.14), channel_id=1, source_target_pairs={{0,16},{8,0},{16,8},{1,17},{9,1},{17,9},{2,18},{10,2},{18,10},{3,1... | collective-permute-start | bytes 1572872 | tf_op jit(solution)/shard_map/ppermute | solution.py:303
  65.3 32.7 %collective-permute-start.6 = (bf16[128,2048]{1,0:T(8,128)(2,1)}, bf16[128,2048]{1,0:T(8,128)(2,1)S(1)}, u32[]{:S(2)}, u32[]{:S(2)}) collective-permute-start(bf16[128,2048]{1,0:T(8,128)(2,1)} %get-tuple-element.15), channel_id=1, source_target_pairs={{0,8},{8,16},{16,0},{1,9},{9,17},{17,1},{2,10},{10,18},{18,2},{3,1... | collective-permute-start | bytes 1572872 | tf_op jit(solution)/shard_map/ppermute | solution.py:303
  69.4 39.9 %collective-permute-start.7 = (bf16[128,2048]{1,0:T(8,128)(2,1)}, bf16[128,2048]{1,0:T(8,128)(2,1)S(1)}, u32[]{:S(2)}, u32[]{:S(2)}) collective-permute-start(bf16[128,2048]{1,0:T(8,128)(2,1)} %get-tuple-element.15), channel_id=1, source_target_pairs={{0,16},{8,0},{16,8},{1,17},{9,1},{17,9},{2,18},{10,2},{18,10},{3,1... | collective-permute-start | bytes 1572872 | tf_op jit(solution)/shard_map/ppermute | solution.py:303
  91.4 23.2 %collective-permute-start.8 = (bf16[384,2048]{1,0:T(8,128)(2,1)S(1)}, bf16[384,2048]{1,0:T(8,128)(2,1)}, u32[]{:S(2)}, u32[]{:S(2)}) collective-permute-start(bf16[384,2048]{1,0:T(8,128)(2,1)S(1)} %constant_dynamic-update-slice_fusion.refs_0_.c), channel_id=1, source_target_pairs={{0,4},{4,0},{1,5},{5,1},{2,6},{6,2},{3,7},{7,3},{8,12},{12,8},{9,1... | collective-permute-start | bytes 4718600 | tf_op jit(solution)/shard_map/ppermute | solution.py:307
  109.3 45.8 %collective-permute-start.9 = (bf16[384,2048]{1,0:T(8,128)(2,1)S(1)}, bf16[384,2048]{1,0:T(8,128)(2,1)}, u32[]{:S(2)}, u32[]{:S(2)}) collective-permute-start(bf16[384,2048]{1,0:T(8,128)(2,1)S(1)} %constant_dynamic-update-slice_fusion.3.refs_1_.c), channel_id=1, source_target_pairs={{0,4},{4,0},{1,5},{5,1},{2,6},{6,2},{3,7},{7,3},{8,12},{12,8},{9,1... | collective-permute-start | bytes 4718600 | tf_op jit(solution)/shard_map/ppermute | solution.py:307
  119.2 14.3 %collective-permute-start.16 = (bf16[384,512]{1,0:T(8,128)(2,1)}, bf16[384,512]{1,0:T(8,128)(2,1)S(1)}, u32[]{:S(2)}, u32[]{:S(2)}) collective-permute-start(bf16[384,512]{1,0:T(8,128)(2,1)} %get-tuple-element.19), channel_id=1, source_target_pairs={{0,24},{24,48},{48,72},{72,0},{1,25},{25,49},{49,73},{73,1},{2,26}... | collective-permute-start | bytes 1179656 | tf_op jit(solution)/shard_map/ppermute | solution.py:311
  122.6 20.3 %collective-permute-start.17 = (bf16[384,512]{1,0:T(8,128)(2,1)}, bf16[384,512]{1,0:T(8,128)(2,1)S(1)}, u32[]{:S(2)}, u32[]{:S(2)}) collective-permute-start(bf16[384,512]{1,0:T(8,128)(2,1)} %get-tuple-element.20), channel_id=1, source_target_pairs={{0,48},{24,72},{48,0},{72,24},{1,49},{25,73},{49,1},{73,25},{2,50}... | collective-permute-start | bytes 1179656 | tf_op jit(solution)/shard_map/ppermute | solution.py:311
  127.2 17.3 %collective-permute-start.18 = (bf16[384,512]{1,0:T(8,128)(2,1)}, bf16[384,512]{1,0:T(8,128)(2,1)S(1)}, u32[]{:S(2)}, u32[]{:S(2)}) collective-permute-start(bf16[384,512]{1,0:T(8,128)(2,1)} %get-tuple-element.21), channel_id=1, source_target_pairs={{0,72},{24,0},{48,24},{72,48},{1,73},{25,1},{49,25},{73,49},{2,74}... | collective-permute-start | bytes 1179656 | tf_op jit(solution)/shard_map/ppermute | solution.py:311
  147.6 39.7 %all-to-all-start.1 = ((bf16[8,4,48,128]{3,2,1,0:T(8,128)(2,1)}), bf16[8,4,48,128]{3,2,1,0:T(8,128)(2,1)S(1)}, u32[]{:S(2)}, u32[]{:S(2)}) async-start(bf16[8,4,48,128]{3,2,1,0:T(8,128)(2,1)} %sum_split.2), calls=%async_computation.1 | async-start | bytes 786432 | tf_op jit(solution)/shard_map/all_to_all | solution.py:315
  164.0 18.8 %collective-permute-start.20 = (bf16[384,512]{1,0:T(8,128)(2,1)}, bf16[384,512]{1,0:T(8,128)(2,1)S(1)}, u32[]{:S(2)}, u32[]{:S(2)}) collective-permute-start(bf16[384,512]{1,0:T(8,128)(2,1)} %get-tuple-element.24), channel_id=1, source_target_pairs={{0,48},{24,72},{48,0},{72,24},{1,49},{25,73},{49,1},{73,25},{2,50}... | collective-permute-start | bytes 1179656 | tf_op jit(solution)/shard_map/ppermute | solution.py:311
  167.6 16.5 %collective-permute-start.21 = (bf16[384,512]{1,0:T(8,128)(2,1)}, bf16[384,512]{1,0:T(8,128)(2,1)S(1)}, u32[]{:S(2)}, u32[]{:S(2)}) collective-permute-start(bf16[384,512]{1,0:T(8,128)(2,1)} %get-tuple-element.25), channel_id=1, source_target_pairs={{0,72},{24,0},{48,24},{72,48},{1,73},{25,1},{49,25},{73,49},{2,74}... | collective-permute-start | bytes 1179656 | tf_op jit(solution)/shard_map/ppermute | solution.py:311
  208.8 29.0 %all-to-all-start.3 = ((bf16[4,2,48,128]{3,2,1,0:T(8,128)(2,1)}), bf16[4,2,48,128]{3,2,1,0:T(8,128)(2,1)S(1)}, u32[]{:S(2)}, u32[]{:S(2)}) async-start(bf16[4,2,48,128]{3,2,1,0:T(8,128)(2,1)} %sum_rows.1), calls=%async_computation.3 | async-start | bytes 196608 | tf_op jit(solution)/shard_map/all_to_all | solution.py:317
  214.6 18.5 %collective-permute-start.10 = (bf16[48,256]{1,0:T(8,128)(2,1)S(1)}, bf16[48,256]{1,0:T(8,128)(2,1)S(1)}, u32[]{:S(2)}, u32[]{:S(2)}) collective-permute-start(bf16[48,256]{1,0:T(8,128)(2,1)S(1)} %dynamic_slice.19.refs_0_), channel_id=1, source_target_pairs={{0,1},{1,2},{2,3},{3,0},{4,5},{5,6},{6,7},{7,4},{8,9},{9,10},{10,1... | collective-permute-start | bytes 73736 | tf_op jit(solution)/shard_map/ppermute | solution.py:292
  237.9 22.6 %all-to-all-start = ((bf16[8,4,48,256]{3,2,1,0:T(8,128)(2,1)}), bf16[8,4,48,256]{3,2,1,0:T(8,128)(2,1)S(1)}, u32[]{:S(2)}, u32[]{:S(2)}) async-start(bf16[8,4,48,256]{3,2,1,0:T(8,128)(2,1)} %spread_cols.1), calls=%async_computation | async-start | bytes 1572864 | tf_op jit(solution)/shard_map/all_to_all | solution.py:294
  260.4 19.6 %all-to-all-start.4 = ((bf16[8,2,48,128]{3,2,1,0:T(8,128)(2,1)}), bf16[8,2,48,128]{3,2,1,0:T(8,128)(2,1)S(1)}, u32[]{:S(2)}, u32[]{:S(2)}) async-start(bf16[8,2,48,128]{3,2,1,0:T(8,128)(2,1)} %spread_sum.1), calls=%async_computation.4 | async-start | bytes 393216 | tf_op jit(solution)/shard_map/all_to_all | solution.py:319
  267.4 36.0 %collective-permute-start.13 = (bf16[384,1024]{1,0:T(8,128)(2,1)}, bf16[384,1024]{1,0:T(8,128)(2,1)S(1)}, u32[]{:S(2)}, u32[]{:S(2)}) collective-permute-start(bf16[384,1024]{1,0:T(8,128)(2,1)} %weight_rows.1.refs_4_), channel_id=1, source_target_pairs={{0,24},{24,48},{48,72},{72,0},{1,25},{25,49},{49,73},{73,1},{2,26}... | collective-permute-start | bytes 2359304 | tf_op jit(solution)/shard_map/ppermute | solution.py:296
  273.5 36.8 %collective-permute-start.14 = (bf16[384,1024]{1,0:T(8,128)(2,1)}, bf16[384,1024]{1,0:T(8,128)(2,1)S(1)}, u32[]{:S(2)}, u32[]{:S(2)}) collective-permute-start(bf16[384,1024]{1,0:T(8,128)(2,1)} %weight_rows.1.refs_4_), channel_id=1, source_target_pairs={{0,48},{24,72},{48,0},{72,24},{1,49},{25,73},{49,1},{73,25},{2,50}... | collective-permute-start | bytes 2359304 | tf_op jit(solution)/shard_map/ppermute | solution.py:296
  277.2 34.5 %collective-permute-start.15 = (bf16[384,1024]{1,0:T(8,128)(2,1)}, bf16[384,1024]{1,0:T(8,128)(2,1)S(1)}, u32[]{:S(2)}, u32[]{:S(2)}) collective-permute-start(bf16[384,1024]{1,0:T(8,128)(2,1)} %weight_rows.1.refs_4_), channel_id=1, source_target_pairs={{0,72},{24,0},{48,24},{72,48},{1,73},{25,1},{49,25},{73,49},{2,74}... | collective-permute-start | bytes 2359304 | tf_op jit(solution)/shard_map/ppermute | solution.py:296
  282.6 39.7 %all-to-all-start.5 = ((bf16[4,2,384,128]{3,2,1,0:T(8,128)(2,1)}), bf16[4,2,384,128]{3,2,1,0:T(8,128)(2,1)S(1)}, u32[]{:S(2)}, u32[]{:S(2)}) async-start(bf16[4,2,384,128]{3,2,1,0:T(8,128)(2,1)} %spread_rows.1), calls=%async_computation.5 | async-start | bytes 1572864 | tf_op jit(solution)/shard_map/all_to_all | solution.py:321
  (28 other events, 219.6 us)

commit v3 on v2

--- a/solution.py
+++ b/solution.py
@@ -137,6 +137,25 @@
         out_specs=[VMEM] * X,
         name="weight_part",
     )(at.reshape(1), *heads_t, own, oth)
+
+
+def weight_stack(heads_t, own, oth):
+    hid = heads_t[0].shape[0]
+    n = ZH * LANE
+
+    def kernel(a, b, c, d, out):
+        for x in range(X):
+            acc = jnp.dot(a[...], c[:, x * n:(x + 1) * n], preferred_element_type=jnp.float32)
+            acc += jnp.dot(b[...], d[:, x * n:(x + 1) * n], preferred_element_type=jnp.float32)
+            out[x] = acc.astype(out.dtype)
+
+    return pl.pallas_call(
+        kernel,
+        out_shape=jax.ShapeDtypeStruct((X, hid, n), own.dtype),
+        in_specs=[VMEM] * 4,
+        out_specs=VMEM,
+        name="weight_stack",
+    )(*heads_t, own, oth)
 
 
 def heads_grad(owns, oths, weights, rows, at):
@@ -175,45 +194,47 @@
     )(at.reshape(1), jnp.stack([r for group in rows for r in group]), *owns, *oths, *weights)
 
 
-def sum_split(parts):
+def sum_first(parts):
+    hid = parts.shape[1]
+    rows = hid // Y
+
+    def kernel(src, out):
+        for y in range(Y):
+            for col in range(ZH):
+                v = src[:, y * rows:(y + 1) * rows, col * LANE:(col + 1) * LANE].astype(jnp.float32)
+                out[y, col] = jnp.sum(v, axis=0).astype(out.dtype)
+
+    return pl.pallas_call(
+        kernel,
+        out_shape=jax.ShapeDtypeStruct((Y, ZH, rows, LANE), parts.dtype),
+        in_specs=[VMEM],
+        out_specs=VMEM,
+        name="sum_first",
+    )(parts)
+
+
+def sum_second(parts, first):
     hid = parts[0].shape[0]
     rows = hid // Y
 
     def kernel(*refs):
-        out = refs[-1]
+        before, out = refs[-2:]
         for y in range(Y):
             for col in range(ZH):
                 total = None
-                for ref in refs[:-1]:
+                for ref in refs[:-2]:
                     v = ref[y * rows:(y + 1) * rows, col * LANE:(col + 1) * LANE].astype(jnp.float32)
                     total = v if total is None else total + v
-                out[y, col] = total.astype(out.dtype)
-
-    return pl.pallas_call(
-        kernel,
-        out_shape=jax.ShapeDtypeStruct((Y, ZH, rows, LANE), parts[0].dtype),
-        in_specs=[VMEM] * len(parts),
-        out_specs=VMEM,
-        name="sum_split",
-    )(*parts)
-
-
-def sum_rows(parts):
-    _, _, rows, _ = parts[0].shape
-
-    def kernel(*refs):
-        out = refs[-1]
-        for h in range(CHUNKS):
-            for col in range(ZH):
-                out[col, h] = jnp.sum(refs[h][:, col].astype(jnp.float32), axis=0).astype(out.dtype)
-
-    return pl.pallas_call(
-        kernel,
-        out_shape=jax.ShapeDtypeStruct((ZH, CHUNKS, rows, LANE), parts[0].dtype),
-        in_specs=[VMEM] * CHUNKS,
-        out_specs=VMEM,
-        name="sum_rows",
-    )(*parts)
+                out[y, col, 0] = before[y, col]
+                out[y, col, 1] = total.astype(out.dtype)
+
+    return pl.pallas_call(
+        kernel,
+        out_shape=jax.ShapeDtypeStruct((Y, ZH, CHUNKS, rows, LANE), parts[0].dtype),
+        in_specs=[VMEM] * (X + 1),
+        out_specs=VMEM,
+        name="sum_second",
+    )(*parts, first)
 
 
 def spread_sum(parts):
@@ -301,20 +322,19 @@
     near = []
     for h in range(CHUNKS):
         near.append([mine[h]] + [lax.ppermute(mine[h], "zl", ring(ZL, k)) for k in (1, 2)])
-    parts, owns, oths = [], [], []
+    owns, oths = [], []
     for h in range(CHUNKS):
         own = jnp.concatenate(near[h], axis=0)
         oth = lax.ppermute(own, "core", ring(CORE, 1))
         owns.append(own)
         oths.append(oth)
-        part = weight_part(heads_t, own, oth, xi)
-        parts.append([part[0]] + [lax.ppermute(part[k], "x", ring(X, k)) for k in range(1, X)])
-    sums = []
-    for h in range(CHUNKS):
-        r = sum_split(parts[h])
-        sums.append(lax.all_to_all(r, "y", 0, 0))
-    r = sum_rows(sums)
-    r = lax.all_to_all(r, "zh", 0, 0)
+    part = weight_stack(heads_t, owns[0], oths[0])
+    part = lax.all_to_all(part, "x", 0, 0)
+    first = sum_first(part)
+    part = weight_part(heads_t, owns[1], oths[1], xi)
+    part = [part[0]] + [lax.ppermute(part[k], "x", ring(X, k)) for k in range(1, X)]
+    r = sum_second(part, first)
+    r = lax.all_to_all(r.reshape((Y * ZH,) + r.shape[2:]), ("y", "zh"), 0, 0)
     r = spread_sum(r)
     r = lax.all_to_all(r, "y", 0, 0)
     r = spread_rows(r)

time: 327 us -> 307 us (0.939)
  the two profiles are of different devices: /device:TPU:8 before, /device:TPU:136 now
where the time goes in v3:
time: 307 us; the launch traced here: 306 us
  waiting for transfers between devices  140 us (46%)
  starting transfers between devices  116 us (38%)
  Pallas kernels  38.7 us (13%)
  local copies, waits for them, and re-layouts  9.95 us (3%)
    ppermute x4, waiting for transfers between devices, per_device(): lax.ppermute(mine[h], 'zl', ring(ZL, k))  38 us
    ppermute x3, waiting for transfers between devices, per_device(): w_x = [w_y] + [lax.ppermute(w_y, 'x', ring(X, k)) for k in range(1, X)]  27.6 us
    ppermute x4, starting transfers between devices, per_device(): lax.ppermute(sends[k], ('zl', 'core', 'zh'), spread_pairs(k))  25.7 us
    ppermute x4, waiting for transfers between devices, per_device(): lax.ppermute(sends[k], ('zl', 'core', 'zh'), spread_pairs(k))  20.7 us
    all_to_all x1, waiting for transfers between devices, per_device(): w_y = lax.all_to_all(w_y, 'y', 0, 0)  19.9 us
    ppermute x3, starting transfers between devices, per_device(): w_far = [lax.ppermute(w_part, 'zh', ring(ZH, k)) for k in range(1, ZH)]  19.1 us
    ppermute x4, starting transfers between devices, per_device(): lax.ppermute(mine[h], 'zl', ring(ZL, k))  18.1 us
    ppermute x3, waiting for transfers between devices, per_device(): w_far = [lax.ppermute(w_part, 'zh', ring(ZH, k)) for k in range(1, ZH)]  15.3 us
  transfers between devices with their start and end apart: 24, of which 14 were waited for; matrix products, arithmetic and copies ran while one was open for 1% of the time, Pallas kernels for 10%

profile of v3, /device:TPU:136, one launch (start us, length us, event | category | flops | bytes accessed | tf_op | source)
XLA Modules:
  0.0 306.0 jit_solution(17727398753231419533)
XLA Ops:
  2.0 12.7 %collective-permute-start = (bf16[128,1024]{1,0:T(8,128)(2,1)S(1)}, bf16[128,1024]{1,0:T(8,128)(2,1)S(1)}, u32[]{:S(2)}, u32[]{:S(2)}) collective-permute-start(bf16[128,1024]{1,0:T(8,128)(2,1)S(1)} %get-tuple-element.20), channel_id=1, source_target_pairs={{0,0},{1,4},{2,8},{3,12},{4,16},{5,20},{6,1},{7,5},{8,9},{9,13},{1... | collective-permute-start | bytes 786440 | tf_op jit(solution)/shard_map/ppermute | solution.py:309
  14.7 4.9 %collective-permute-start.1 = (bf16[128,1024]{1,0:T(8,128)(2,1)S(1)}, bf16[128,1024]{1,0:T(8,128)(2,1)S(1)}, u32[]{:S(2)}, u32[]{:S(2)}) collective-permute-start(bf16[128,1024]{1,0:T(8,128)(2,1)S(1)} %get-tuple-element.19), channel_id=1, source_target_pairs={{0,4},{1,8},{2,12},{3,0},{4,20},{5,1},{6,5},{7,16},{8,13},{9,17},{... | collective-permute-start | bytes 786440 | tf_op jit(solution)/shard_map/ppermute | solution.py:309
  21.6 6.1 %collective-permute-start.3 = (bf16[128,1024]{1,0:T(8,128)(2,1)S(1)}, bf16[128,1024]{1,0:T(8,128)(2,1)S(1)}, u32[]{:S(2)}, u32[]{:S(2)}) collective-permute-start(bf16[128,1024]{1,0:T(8,128)(2,1)S(1)} %get-tuple-element.18), channel_id=1, source_target_pairs={{0,12},{1,0},{2,4},{3,8},{4,5},{5,16},{6,20},{7,1},{8,21},{9,9},{1... | collective-permute-start | bytes 786440 | tf_op jit(solution)/shard_map/ppermute | solution.py:309
  27.7 17.6 %collective-permute-done.1.refs_1_ = bf16[128,1024]{1,0:T(8,128)(2,1)S(1)} collective-permute-done((bf16[128,1024]{1,0:T(8,128)(2,1)S(1)}, bf16[128,1024]{1,0:T(8,128)(2,1)S(1)}, u32[]{:S(2)}, u32[]{:S(2)}) %collective-permute-start.1) | collective-permute-done | bytes 262176 | tf_op jit(solution)/shard_map/ppermute | solution.py:309
  53.5 9.1 %collective-permute-start.5 = (bf16[128,2048]{1,0:T(8,128)(2,1)}, bf16[128,2048]{1,0:T(8,128)(2,1)S(1)}, u32[]{:S(2)}, u32[]{:S(2)}) collective-permute-start(bf16[128,2048]{1,0:T(8,128)(2,1)} %get-tuple-element.10), channel_id=1, source_target_pairs={{0,16},{8,0},{16,8},{1,17},{9,1},{17,9},{2,18},{10,2},{18,10},{3,1... | collective-permute-start | bytes 1572872 | tf_op jit(solution)/shard_map/ppermute | solution.py:324
  67.2 6.4 %collective-permute-done.4 = bf16[128,2048]{1,0:T(8,128)(2,1)S(1)} collective-permute-done((bf16[128,2048]{1,0:T(8,128)(2,1)}, bf16[128,2048]{1,0:T(8,128)(2,1)S(1)}, u32[]{:S(2)}, u32[]{:S(2)}) %collective-permute-start.4) | collective-permute-done | bytes 524320 | tf_op jit(solution)/shard_map/ppermute | solution.py:324
  73.7 12.3 %collective-permute-done.5 = bf16[128,2048]{1,0:T(8,128)(2,1)S(1)} collective-permute-done((bf16[128,2048]{1,0:T(8,128)(2,1)}, bf16[128,2048]{1,0:T(8,128)(2,1)S(1)}, u32[]{:S(2)}, u32[]{:S(2)}) %collective-permute-start.5) | collective-permute-done | bytes 524320 | tf_op jit(solution)/shard_map/ppermute | solution.py:324
  95.8 15.9 %collective-permute-done.7 = bf16[128,2048]{1,0:T(8,128)(2,1)S(1)} collective-permute-done((bf16[128,2048]{1,0:T(8,128)(2,1)S(1)}, bf16[128,2048]{1,0:T(8,128)(2,1)S(1)}, u32[]{:S(2)}, u32[]{:S(2)}) %collective-permute-start.7) | collective-permute-done | bytes 524320 | tf_op jit(solution)/shard_map/ppermute | solution.py:324
  116.5 5.0 %weight_stack.1 = bf16[4,384,512]{2,1,0:T(8,128)(2,1)} custom-call(bf16[384,384]{1,0:T(8,128)(2,1)} %get-tuple-element.12.a, bf16[384,384]{1,0:T(8,128)(2,1)} %get-tuple-element.13.b, bf16[384,2048]{1,0:T(8,128)(2,1)} %copy-done.1, bf16[384,2048]{1,0:T(8,128)(2,1)} %collective-permute-done.8.refs_2_.d), custom_call_target="tpu_custom_call" | custom-call | tf_op jit(solution)/shard_map/weight_stack/pallas_call | solution.py:152
  125.8 4.6 %weight_part.1 = (bf16[384,512]{1,0:T(8,128)(2,1)}, bf16[384,512]{1,0:T(8,128)(2,1)}, bf16[384,512]{1,0:T(8,128)(2,1)}, bf16[384,512]{1,0:T(8,128)(2,1)}) custom-call(s32[1]{0:T(128)} %bitcast.at_ref, bf16[384,384]{1,0:T(8,128)(2,1)} %get-tuple-element.12.a, bf16[384,384]{1,0:T(8,128)(2,1)} %get-tuple-element.13.b, bf16[384,2048]{1,0:T(8,128)(2,1)} %copy-done, ...), custom_call_target="tpu_custom_call" | custom-call | tf_op jit(solution)/shard_map/weight_part/pallas_call | solution.py:133
  134.4 4.6 %collective-permute-start.17 = (bf16[384,512]{1,0:T(8,128)(2,1)}, bf16[384,512]{1,0:T(8,128)(2,1)S(1)}, u32[]{:S(2)}, u32[]{:S(2)}) collective-permute-start(bf16[384,512]{1,0:T(8,128)(2,1)} %get-tuple-element.16), channel_id=1, source_target_pairs={{0,48},{24,72},{48,0},{72,24},{1,49},{25,73},{49,1},{73,25},{2,50}... | collective-permute-start | bytes 1179656 | tf_op jit(solution)/shard_map/ppermute | solution.py:335
  142.4 5.6 %all-to-all-done.1.src = bf16[4,384,512]{2,1,0:T(8,128)(2,1)S(1)} async-done(((bf16[4,384,512]{2,1,0:T(8,128)(2,1)}), bf16[4,384,512]{2,1,0:T(8,128)(2,1)S(1)}, u32[]{:S(2)}, u32[]{:S(2)}) %all-to-all-start.1) | async-done | bytes 1572896 | tf_op jit(solution)/shard_map/all_to_all | solution.py:332
  155.8 8.4 %collective-permute-done.17.refs_2_ = bf16[384,512]{1,0:T(8,128)(2,1)S(1)} collective-permute-done((bf16[384,512]{1,0:T(8,128)(2,1)}, bf16[384,512]{1,0:T(8,128)(2,1)S(1)}, u32[]{:S(2)}, u32[]{:S(2)}) %collective-permute-start.17) | collective-permute-done | bytes 393248 | tf_op jit(solution)/shard_map/ppermute | solution.py:335
  167.5 7.7 %all-to-all-start.2 = ((bf16[32,2,48,128]{3,2,1,0:T(8,128)(2,1)}), bf16[32,2,48,128]{3,2,1,0:T(8,128)(2,1)S(1)}, u32[]{:S(2)}, u32[]{:S(2)}) async-start(bf16[32,2,48,128]{3,2,1,0:T(8,128)(2,1)} %bitcast.10), calls=%async_computation.2 | async-start | bytes 1572864 | tf_op jit(solution)/shard_map/all_to_all | solution.py:337
  176.0 6.4 %collective-permute-start.10 = (bf16[48,256]{1,0:T(8,128)(2,1)S(1)}, bf16[48,256]{1,0:T(8,128)(2,1)S(1)}, u32[]{:S(2)}, u32[]{:S(2)}) collective-permute-start(bf16[48,256]{1,0:T(8,128)(2,1)S(1)} %dynamic_slice.19.refs_0_), channel_id=1, source_target_pairs={{0,1},{1,2},{2,3},{3,0},{4,5},{5,6},{6,7},{7,4},{8,9},{9,10},{10,1... | collective-permute-start | bytes 73736 | tf_op jit(solution)/shard_map/ppermute | solution.py:313
  182.4 5.2 %collective-permute-start.11 = (bf16[48,256]{1,0:T(8,128)(2,1)S(1)}, bf16[48,256]{1,0:T(8,128)(2,1)S(1)}, u32[]{:S(2)}, u32[]{:S(2)}) collective-permute-start(bf16[48,256]{1,0:T(8,128)(2,1)S(1)} %dynamic_slice.19.refs_0_), channel_id=1, source_target_pairs={{0,2},{1,3},{2,0},{3,1},{4,6},{5,7},{6,4},{7,5},{8,10},{9,11},{10,... | collective-permute-start | bytes 73736 | tf_op jit(solution)/shard_map/ppermute | solution.py:313
  187.6 7.5 %collective-permute-start.12 = (bf16[48,256]{1,0:T(8,128)(2,1)S(1)}, bf16[48,256]{1,0:T(8,128)(2,1)S(1)}, u32[]{:S(2)}, u32[]{:S(2)}) collective-permute-start(bf16[48,256]{1,0:T(8,128)(2,1)S(1)} %dynamic_slice.19.refs_0_), channel_id=1, source_target_pairs={{0,3},{1,0},{2,1},{3,2},{4,7},{5,4},{6,5},{7,6},{8,11},{9,8},{10,9... | collective-permute-start | bytes 73736 | tf_op jit(solution)/shard_map/ppermute | solution.py:313
  195.2 8.3 %collective-permute-done.10.refs_1_ = bf16[48,256]{1,0:T(8,128)(2,1)S(1)} collective-permute-done((bf16[48,256]{1,0:T(8,128)(2,1)S(1)}, bf16[48,256]{1,0:T(8,128)(2,1)S(1)}, u32[]{:S(2)}, u32[]{:S(2)}) %collective-permute-start.10) | collective-permute-done | bytes 24608 | tf_op jit(solution)/shard_map/ppermute | solution.py:313
  203.5 7.0 %collective-permute-done.11.refs_2_ = bf16[48,256]{1,0:T(8,128)(2,1)S(1)} collective-permute-done((bf16[48,256]{1,0:T(8,128)(2,1)S(1)}, bf16[48,256]{1,0:T(8,128)(2,1)S(1)}, u32[]{:S(2)}, u32[]{:S(2)}) %collective-permute-start.11) | collective-permute-done | bytes 24608 | tf_op jit(solution)/shard_map/ppermute | solution.py:313
  212.9 7.2 %all-to-all-start = ((bf16[8,4,48,256]{3,2,1,0:T(8,128)(2,1)}), bf16[8,4,48,256]{3,2,1,0:T(8,128)(2,1)S(1)}, u32[]{:S(2)}, u32[]{:S(2)}) async-start(bf16[8,4,48,256]{3,2,1,0:T(8,128)(2,1)} %spread_cols.1), calls=%async_computation | async-start | bytes 1572864 | tf_op jit(solution)/shard_map/all_to_all | solution.py:315
  222.0 19.9 %all-to-all-done.src = bf16[8,4,48,256]{3,2,1,0:T(8,128)(2,1)S(1)} async-done(((bf16[8,4,48,256]{3,2,1,0:T(8,128)(2,1)}), bf16[8,4,48,256]{3,2,1,0:T(8,128)(2,1)S(1)}, u32[]{:S(2)}, u32[]{:S(2)}) %all-to-all-start) | async-done | bytes 786464 | tf_op jit(solution)/shard_map/all_to_all | solution.py:315
  242.0 4.8 %all-to-all-start.3 = ((bf16[8,2,48,128]{3,2,1,0:T(8,128)(2,1)}), bf16[8,2,48,128]{3,2,1,0:T(8,128)(2,1)S(1)}, u32[]{:S(2)}, u32[]{:S(2)}) async-start(bf16[8,2,48,128]{3,2,1,0:T(8,128)(2,1)} %spread_sum.1), calls=%async_computation.3 | async-start | bytes 393216 | tf_op jit(solution)/shard_map/all_to_all | solution.py:339
  264.6 24.8 %collective-permute-done.13.refs_5_ = bf16[384,1024]{1,0:T(8,128)(2,1)S(1)} collective-permute-done((bf16[384,1024]{1,0:T(8,128)(2,1)}, bf16[384,1024]{1,0:T(8,128)(2,1)S(1)}, u32[]{:S(2)}, u32[]{:S(2)}) %collective-permute-start.13) | collective-permute-done | bytes 786464 | tf_op jit(solution)/shard_map/ppermute | solution.py:317
  293.2 9.6 %heads_grad.1 = bf16[768,384]{1,0:T(8,128)(2,1)} custom-call(s32[1]{0:T(128)} %bitcast.at_ref, s32[6]{0:T(128)} %stack.34.rows_ref, bf16[384,2048]{1,0:T(8,128)(2,1)} %copy-done.1, bf16[384,2048]{1,0:T(8,128)(2,1)} %copy-done, bf16[384,2048]{1,0:T(8,128)(2,1)} %collective-permute-done.8.refs_2_.d, bf16[384,2048]{1,0:T(8,128)(2,1)} %collective-permute-done.9.refs_3_.d, ...), custom_call_target="tpu_custom_call" | custom-call | tf_op jit(solution)/shard_map/heads_grad/pallas_call | solution.py:187
  (89 shorter events, 83.3 us)
Async XLA Ops:
  2.0 25.7 %collective-permute-start = (bf16[128,1024]{1,0:T(8,128)(2,1)S(1)}, bf16[128,1024]{1,0:T(8,128)(2,1)S(1)}, u32[]{:S(2)}, u32[]{:S(2)}) collective-permute-start(bf16[128,1024]{1,0:T(8,128)(2,1)S(1)} %get-tuple-element.20), channel_id=1, source_target_pairs={{0,0},{1,4},{2,8},{3,12},{4,16},{5,20},{6,1},{7,5},{8,9},{9,13},{1... | collective-permute-start | bytes 786440 | tf_op jit(solution)/shard_map/ppermute | solution.py:309
  14.7 30.6 %collective-permute-start.1 = (bf16[128,1024]{1,0:T(8,128)(2,1)S(1)}, bf16[128,1024]{1,0:T(8,128)(2,1)S(1)}, u32[]{:S(2)}, u32[]{:S(2)}) collective-permute-start(bf16[128,1024]{1,0:T(8,128)(2,1)S(1)} %get-tuple-element.19), channel_id=1, source_target_pairs={{0,4},{1,8},{2,12},{3,0},{4,20},{5,1},{6,5},{7,16},{8,13},{9,17},{... | collective-permute-start | bytes 786440 | tf_op jit(solution)/shard_map/ppermute | solution.py:309
  19.6 28.7 %collective-permute-start.2 = (bf16[128,1024]{1,0:T(8,128)(2,1)S(1)}, bf16[128,1024]{1,0:T(8,128)(2,1)S(1)}, u32[]{:S(2)}, u32[]{:S(2)}) collective-permute-start(bf16[128,1024]{1,0:T(8,128)(2,1)S(1)} %get-tuple-element.21), channel_id=1, source_target_pairs={{0,8},{1,12},{2,0},{3,4},{4,1},{5,5},{6,16},{7,20},{8,17},{9,21},{... | collective-permute-start | bytes 786440 | tf_op jit(solution)/shard_map/ppermute | solution.py:309
  21.6 26.8 %collective-permute-start.3 = (bf16[128,1024]{1,0:T(8,128)(2,1)S(1)}, bf16[128,1024]{1,0:T(8,128)(2,1)S(1)}, u32[]{:S(2)}, u32[]{:S(2)}) collective-permute-start(bf16[128,1024]{1,0:T(8,128)(2,1)S(1)} %get-tuple-element.18), channel_id=1, source_target_pairs={{0,12},{1,0},{2,4},{3,8},{4,5},{5,16},{6,20},{7,1},{8,21},{9,9},{1... | collective-permute-start | bytes 786440 | tf_op jit(solution)/shard_map/ppermute | solution.py:309
  51.6 22.0 %collective-permute-start.4 = (bf16[128,2048]{1,0:T(8,128)(2,1)}, bf16[128,2048]{1,0:T(8,128)(2,1)S(1)}, u32[]{:S(2)}, u32[]{:S(2)}) collective-permute-start(bf16[128,2048]{1,0:T(8,128)(2,1)} %get-tuple-element.10), channel_id=1, source_target_pairs={{0,8},{8,16},{16,0},{1,9},{9,17},{17,1},{2,10},{10,18},{18,2},{3,1... | collective-permute-start | bytes 1572872 | tf_op jit(solution)/shard_map/ppermute | solution.py:324
  53.5 32.4 %collective-permute-start.5 = (bf16[128,2048]{1,0:T(8,128)(2,1)}, bf16[128,2048]{1,0:T(8,128)(2,1)S(1)}, u32[]{:S(2)}, u32[]{:S(2)}) collective-permute-start(bf16[128,2048]{1,0:T(8,128)(2,1)} %get-tuple-element.10), channel_id=1, source_target_pairs={{0,16},{8,0},{16,8},{1,17},{9,1},{17,9},{2,18},{10,2},{18,10},{3,1... | collective-permute-start | bytes 1572872 | tf_op jit(solution)/shard_map/ppermute | solution.py:324
  62.6 33.2 %collective-permute-start.6 = (bf16[128,2048]{1,0:T(8,128)(2,1)}, bf16[128,2048]{1,0:T(8,128)(2,1)S(1)}, u32[]{:S(2)}, u32[]{:S(2)}) collective-permute-start(bf16[128,2048]{1,0:T(8,128)(2,1)} %get-tuple-element.11), channel_id=1, source_target_pairs={{0,8},{8,16},{16,0},{1,9},{9,17},{17,1},{2,10},{10,18},{18,2},{3,1... | collective-permute-start | bytes 1572872 | tf_op jit(solution)/shard_map/ppermute | solution.py:324
  86.0 30.5 %collective-permute-start.8 = (bf16[384,2048]{1,0:T(8,128)(2,1)S(1)}, bf16[384,2048]{1,0:T(8,128)(2,1)}, u32[]{:S(2)}, u32[]{:S(2)}) collective-permute-start(bf16[384,2048]{1,0:T(8,128)(2,1)S(1)} %constant_dynamic-update-slice_fusion.refs_0_.c), channel_id=1, source_target_pairs={{0,4},{4,0},{1,5},{5,1},{2,6},{6,2},{3,7},{7,3},{8,12},{12,8},{9,1... | collective-permute-start | bytes 4718600 | tf_op jit(solution)/shard_map/ppermute | solution.py:328
  88.6 23.1 %collective-permute-start.7 = (bf16[128,2048]{1,0:T(8,128)(2,1)S(1)}, bf16[128,2048]{1,0:T(8,128)(2,1)S(1)}, u32[]{:S(2)}, u32[]{:S(2)}) collective-permute-start(bf16[128,2048]{1,0:T(8,128)(2,1)S(1)} %copy-done.10), channel_id=1, source_target_pairs={{0,16},{8,0},{16,8},{1,17},{9,1},{17,9},{2,18},{10,2},{18,10},{3,1... | collective-permute-start | bytes 1572872 | tf_op jit(solution)/shard_map/ppermute | solution.py:324
  111.8 14.1 %collective-permute-start.9 = (bf16[384,2048]{1,0:T(8,128)(2,1)S(1)}, bf16[384,2048]{1,0:T(8,128)(2,1)}, u32[]{:S(2)}, u32[]{:S(2)}) collective-permute-start(bf16[384,2048]{1,0:T(8,128)(2,1)S(1)} %constant_dynamic-update-slice_fusion.3.refs_1_.c), channel_id=1, source_target_pairs={{0,4},{4,0},{1,5},{5,1},{2,6},{6,2},{3,7},{7,3},{8,12},{12,8},{9,1... | collective-permute-start | bytes 4718600 | tf_op jit(solution)/shard_map/ppermute | solution.py:328
  121.5 26.5 %all-to-all-start.1 = ((bf16[4,384,512]{2,1,0:T(8,128)(2,1)}), bf16[4,384,512]{2,1,0:T(8,128)(2,1)S(1)}, u32[]{:S(2)}, u32[]{:S(2)}) async-start(bf16[4,384,512]{2,1,0:T(8,128)(2,1)} %weight_stack.1), calls=%async_computation.1 | async-start | bytes 3145728 | tf_op jit(solution)/shard_map/all_to_all | solution.py:332
  130.5 25.3 %collective-permute-start.16 = (bf16[384,512]{1,0:T(8,128)(2,1)}, bf16[384,512]{1,0:T(8,128)(2,1)S(1)}, u32[]{:S(2)}, u32[]{:S(2)}) collective-permute-start(bf16[384,512]{1,0:T(8,128)(2,1)} %get-tuple-element.15), channel_id=1, source_target_pairs={{0,24},{24,48},{48,72},{72,0},{1,25},{25,49},{49,73},{73,1},{2,26}... | collective-permute-start | bytes 1179656 | tf_op jit(solution)/shard_map/ppermute | solution.py:335
  134.4 29.7 %collective-permute-start.17 = (bf16[384,512]{1,0:T(8,128)(2,1)}, bf16[384,512]{1,0:T(8,128)(2,1)S(1)}, u32[]{:S(2)}, u32[]{:S(2)}) collective-permute-start(bf16[384,512]{1,0:T(8,128)(2,1)} %get-tuple-element.16), channel_id=1, source_target_pairs={{0,48},{24,72},{48,0},{72,24},{1,49},{25,73},{49,1},{73,25},{2,50}... | collective-permute-start | bytes 1179656 | tf_op jit(solution)/shard_map/ppermute | solution.py:335
  139.0 25.1 %collective-permute-start.18 = (bf16[384,512]{1,0:T(8,128)(2,1)}, bf16[384,512]{1,0:T(8,128)(2,1)S(1)}, u32[]{:S(2)}, u32[]{:S(2)}) collective-permute-start(bf16[384,512]{1,0:T(8,128)(2,1)} %get-tuple-element.17), channel_id=1, source_target_pairs={{0,72},{24,0},{48,24},{72,48},{1,73},{25,1},{49,25},{73,49},{2,74}... | collective-permute-start | bytes 1179656 | tf_op jit(solution)/shard_map/ppermute | solution.py:335
  167.5 45.4 %all-to-all-start.2 = ((bf16[32,2,48,128]{3,2,1,0:T(8,128)(2,1)}), bf16[32,2,48,128]{3,2,1,0:T(8,128)(2,1)S(1)}, u32[]{:S(2)}, u32[]{:S(2)}) async-start(bf16[32,2,48,128]{3,2,1,0:T(8,128)(2,1)} %bitcast.10), calls=%async_computation.2 | async-start | bytes 1572864 | tf_op jit(solution)/shard_map/all_to_all | solution.py:337
  176.0 27.5 %collective-permute-start.10 = (bf16[48,256]{1,0:T(8,128)(2,1)S(1)}, bf16[48,256]{1,0:T(8,128)(2,1)S(1)}, u32[]{:S(2)}, u32[]{:S(2)}) collective-permute-start(bf16[48,256]{1,0:T(8,128)(2,1)S(1)} %dynamic_slice.19.refs_0_), channel_id=1, source_target_pairs={{0,1},{1,2},{2,3},{3,0},{4,5},{5,6},{6,7},{7,4},{8,9},{9,10},{10,1... | collective-permute-start | bytes 73736 | tf_op jit(solution)/shard_map/ppermute | solution.py:313
  182.4 28.1 %collective-permute-start.11 = (bf16[48,256]{1,0:T(8,128)(2,1)S(1)}, bf16[48,256]{1,0:T(8,128)(2,1)S(1)}, u32[]{:S(2)}, u32[]{:S(2)}) collective-permute-start(bf16[48,256]{1,0:T(8,128)(2,1)S(1)} %dynamic_slice.19.refs_0_), channel_id=1, source_target_pairs={{0,2},{1,3},{2,0},{3,1},{4,6},{5,7},{6,4},{7,5},{8,10},{9,11},{10,... | collective-permute-start | bytes 73736 | tf_op jit(solution)/shard_map/ppermute | solution.py:313
  187.6 22.8 %collective-permute-start.12 = (bf16[48,256]{1,0:T(8,128)(2,1)S(1)}, bf16[48,256]{1,0:T(8,128)(2,1)S(1)}, u32[]{:S(2)}, u32[]{:S(2)}) collective-permute-start(bf16[48,256]{1,0:T(8,128)(2,1)S(1)} %dynamic_slice.19.refs_0_), channel_id=1, source_target_pairs={{0,3},{1,0},{2,1},{3,2},{4,7},{5,4},{6,5},{7,6},{8,11},{9,8},{10,9... | collective-permute-start | bytes 73736 | tf_op jit(solution)/shard_map/ppermute | solution.py:313
  212.9 29.1 %all-to-all-start = ((bf16[8,4,48,256]{3,2,1,0:T(8,128)(2,1)}), bf16[8,4,48,256]{3,2,1,0:T(8,128)(2,1)S(1)}, u32[]{:S(2)}, u32[]{:S(2)}) async-start(bf16[8,4,48,256]{3,2,1,0:T(8,128)(2,1)} %spread_cols.1), calls=%async_computation | async-start | bytes 1572864 | tf_op jit(solution)/shard_map/all_to_all | solution.py:315
  242.0 16.4 %all-to-all-start.3 = ((bf16[8,2,48,128]{3,2,1,0:T(8,128)(2,1)}), bf16[8,2,48,128]{3,2,1,0:T(8,128)(2,1)S(1)}, u32[]{:S(2)}, u32[]{:S(2)}) async-start(bf16[8,2,48,128]{3,2,1,0:T(8,128)(2,1)} %spread_sum.1), calls=%async_computation.3 | async-start | bytes 393216 | tf_op jit(solution)/shard_map/all_to_all | solution.py:339
  248.9 40.6 %collective-permute-start.13 = (bf16[384,1024]{1,0:T(8,128)(2,1)}, bf16[384,1024]{1,0:T(8,128)(2,1)S(1)}, u32[]{:S(2)}, u32[]{:S(2)}) collective-permute-start(bf16[384,1024]{1,0:T(8,128)(2,1)} %weight_rows.1.refs_4_), channel_id=1, source_target_pairs={{0,24},{24,48},{48,72},{72,0},{1,25},{25,49},{49,73},{73,1},{2,26}... | collective-permute-start | bytes 2359304 | tf_op jit(solution)/shard_map/ppermute | solution.py:317
  251.8 37.6 %collective-permute-start.14 = (bf16[384,1024]{1,0:T(8,128)(2,1)}, bf16[384,1024]{1,0:T(8,128)(2,1)S(1)}, u32[]{:S(2)}, u32[]{:S(2)}) collective-permute-start(bf16[384,1024]{1,0:T(8,128)(2,1)} %weight_rows.1.refs_4_), channel_id=1, source_target_pairs={{0,48},{24,72},{48,0},{72,24},{1,49},{25,73},{49,1},{73,25},{2,50}... | collective-permute-start | bytes 2359304 | tf_op jit(solution)/shard_map/ppermute | solution.py:317
  255.8 36.5 %collective-permute-start.15 = (bf16[384,1024]{1,0:T(8,128)(2,1)}, bf16[384,1024]{1,0:T(8,128)(2,1)S(1)}, u32[]{:S(2)}, u32[]{:S(2)}) collective-permute-start(bf16[384,1024]{1,0:T(8,128)(2,1)} %weight_rows.1.refs_4_), channel_id=1, source_target_pairs={{0,72},{24,0},{48,24},{72,48},{1,73},{25,1},{49,25},{73,49},{2,74}... | collective-permute-start | bytes 2359304 | tf_op jit(solution)/shard_map/ppermute | solution.py:317
  260.9 41.9 %all-to-all-start.4 = ((bf16[4,2,384,128]{3,2,1,0:T(8,128)(2,1)}), bf16[4,2,384,128]{3,2,1,0:T(8,128)(2,1)S(1)}, u32[]{:S(2)}, u32[]{:S(2)}) async-start(bf16[4,2,384,128]{3,2,1,0:T(8,128)(2,1)} %spread_rows.1), calls=%async_computation.4 | async-start | bytes 1572864 | tf_op jit(solution)/shard_map/all_to_all | solution.py:341
  (22 other events, 160.9 us)
